TPU v7x, 32 devices: a whole 2x2x4 slice. The times are simulated.
32 devices in a mesh: dp: 8 (over y, x, core), mp: 4 (over z).
Axes of the slice: x: 2, y: 2, z: 4, core: 2. Of those that a mesh axis runs over, the one named last changes fastest.
Arguments:
- tokens: bfloat16 [8192, 1152], P('dp'), may hold values from -6 to 6
- cotangent: bfloat16 [8192, 1152], P('dp'), may hold values from -6 to 6
- lengths: int32 [8], P('dp'), may hold values from 512 to 1024, as said below
- rates: float32 [6], replicated, as said below
- query_weight: float32 [1152, 1024], P('dp', 'mp'), may hold values from -0.1875 to 0.1875
- query_moment: float32 [1152, 1024], P('dp', 'mp'), may hold values from -256 to 256
- query_average: float32 [1152, 1024], P('dp', 'mp'), may hold values from -0.1875 to 0.1875
- output_weight: float32 [1024, 1152], P('mp', 'dp'), may hold values from -1.5 to 1.5
- output_moment: float32 [1024, 1152], P('mp', 'dp'), may hold values from -56 to 56
- output_average: float32 [1024, 1152], P('mp', 'dp'), may hold values from -1.5 to 1.5
- gating_weight: float32 [2, 1152, 6912], P(None, 'dp', 'mp'), may hold values from -0.1875 to 0.1875
- gating_moment: float32 [2, 1152, 6912], P(None, 'dp', 'mp'), may hold values from -128 to 128
- gating_average: float32 [2, 1152, 6912], P(None, 'dp', 'mp'), may hold values from -0.1875 to 0.1875
- down_weight: float32 [6912, 1152], P('mp', 'dp'), may hold values from -0.078125 to 0.078125
- down_moment: float32 [6912, 1152], P('mp', 'dp'), may hold values from -256 to 256
- down_average: float32 [6912, 1152], P('mp', 'dp'), may hold values from -0.078125 to 0.078125
- context_weight: float32 [2, 1152, 256], P(None, ('dp', 'mp')), may hold values from -0.1875 to 0.1875
- context_moment: float32 [2, 1152, 256], P(None, ('dp', 'mp')), may hold values from -512 to 512
- context_average: float32 [2, 1152, 256], P(None, ('dp', 'mp')), may hold values from -0.1875 to 0.1875
- gains_weight: float32 [2, 1152], P(None, ('dp', 'mp')), may hold values from 0.5 to 1.5
- gains_moment: float32 [2, 1152], P(None, ('dp', 'mp')), may hold values from -160 to 160
- gains_average: float32 [2, 1152], P(None, ('dp', 'mp')), may hold values from 0.5 to 1.5
Outputs:
- block_out: float32 [8192, 1152], P(('dp', 'mp'))
- tokens_grad: float32 [8192, 1152], P(('dp', 'mp'))
- query_grads: float32 [1152, 1024], P('dp', 'mp')
- query_moments: float32 [1152, 1024], P('dp', 'mp')
- query_averages: float32 [1152, 1024], P('dp', 'mp')
- query_updated: float32 [1152, 1024], P('dp', 'mp')
- output_grads: float32 [1024, 1152], P('mp', 'dp')
- output_moments: float32 [1024, 1152], P('mp', 'dp')
- output_averages: float32 [1024, 1152], P('mp', 'dp')
- output_updated: float32 [1024, 1152], P('mp', 'dp')
- gating_grads: float32 [2, 1152, 6912], P(None, 'dp', 'mp')
- gating_moments: float32 [2, 1152, 6912], P(None, 'dp', 'mp')
- gating_averages: float32 [2, 1152, 6912], P(None, 'dp', 'mp')
- gating_updated: float32 [2, 1152, 6912], P(None, 'dp', 'mp')
- down_grads: float32 [6912, 1152], P('mp', 'dp')
- down_moments: float32 [6912, 1152], P('mp', 'dp')
- down_averages: float32 [6912, 1152], P('mp', 'dp')
- down_updated: float32 [6912, 1152], P('mp', 'dp')
- context_grads: float32 [2, 1152, 256], P(None, ('dp', 'mp'))
- context_moments: float32 [2, 1152, 256], P(None, ('dp', 'mp'))
- context_averages: float32 [2, 1152, 256], P(None, ('dp', 'mp'))
- context_updated: float32 [2, 1152, 256], P(None, ('dp', 'mp'))
- gains_grads: float32 [2, 1152], P(None, ('dp', 'mp'))
- gains_moments: float32 [2, 1152], P(None, ('dp', 'mp'))
- gains_averages: float32 [2, 1152], P(None, ('dp', 'mp'))
- gains_updated: float32 [2, 1152], P(None, ('dp', 'mp'))
Inputs may be any that keep to these rules, and one draw needn't show every extreme that they name: `lengths`: the true token count of each sequence; slots at and after it are padding; at least one sequence fills all 1024 slots. `rates`: one positive learning rate per parameter kind.
All inputs are finite; a program needn't handle non-finite values.
Results may differ from a plain program's by a relative error of at most 0.014.
Values may be sent and summed in bfloat16 or wider, within the bound.
No kernel may reach another device: no remote copies, remote signals or barrier semaphores. Data moves between devices by JAX's collectives and lax.ppermute only.
A program may use at most 192 MiB of HBM per device.

v0:
```python
import jax
import jax.numpy as jnp
from jax import lax
from jax.sharding import PartitionSpec as P

HD = 256


EPSILON = 1e-06
MOMENTUM = 0.9
AVERAGING = 0.5


def rms_norm(tensor, gain_vec):
    return (
        tensor * lax.rsqrt(jnp.mean(tensor * tensor, axis=-1, keepdims=True) + EPSILON) * gain_vec
    )


def normalize(tensor):
    return tensor * lax.rsqrt(jnp.mean(tensor * tensor, axis=-1, keepdims=True) + EPSILON)


def norm_back(grad_in, tensor, gain_vec):

    def apply_norm(inner):
        return rms_norm(inner, gain_vec)

    unused_out, pull = jax.vjp(apply_norm, tensor)
    return pull(grad_in)[0]


def gated_unit(gate_pre, up_pre):
    return jax.nn.gelu(gate_pre, approximate=True) * up_pre


def rotation(length, head_size):
    halfway = head_size // 2
    frequency = 1000000.0 ** (-(jnp.arange(halfway).astype(jnp.float32) * 2.0 / head_size))
    angles = jnp.arange(length).astype(jnp.float32)[:, None] * frequency[None, :]
    return (jnp.cos(angles), jnp.sin(angles))


def rotate(tensor, cosine, sine_tab):
    halfway = tensor.shape[-1] // 2
    former = tensor[..., :halfway]
    latter = tensor[..., halfway:]
    cos_rows = cosine[:, None, :]
    sin_rows = sine_tab[:, None, :]
    return jnp.concatenate(
        [former * cos_rows - latter * sin_rows, latter * cos_rows + former * sin_rows], axis=-1
    )


def advance(gradient, moment, average, weight, step_rate):
    moment_new = MOMENTUM * moment + gradient
    weight_new = weight - step_rate * (gradient + MOMENTUM * moment_new)
    average_new = AVERAGING * average + (1.0 - AVERAGING) * weight_new
    return (gradient, moment_new, average_new, weight_new)


def block_scores(block_query, keys, start, block_rows, length):
    row_count = keys.shape[0]
    places = jnp.arange(row_count, dtype=jnp.int32)
    scores = (
        jnp.einsum("qhd,kd->hqk", block_query, keys, preferred_element_type=jnp.float32) * 0.0625
    )
    rows_here = start + jnp.arange(block_rows, dtype=jnp.int32)
    allowed = (places[None, :] <= rows_here[:, None]) & (places[None, :] < length)
    return jnp.where(allowed[None], scores, -1e30)


def attention_forward(query, keys, values, length, block_rows):
    row_count = keys.shape[0]

    def one_block(start):
        block_query = lax.dynamic_slice_in_dim(query, start, block_rows, 0)
        scores = block_scores(block_query, keys, start, block_rows, length)
        highest = jnp.max(scores, axis=-1, keepdims=True)
        weights = jnp.exp(scores - highest)
        summed = jnp.sum(weights, axis=-1, keepdims=True)
        probs = (weights / summed).astype(jnp.bfloat16)
        mixed = jnp.einsum("hqk,kd->qhd", probs, values, preferred_element_type=jnp.float32)
        return (mixed, highest[..., 0] + jnp.log(summed[..., 0]))

    starts = jnp.arange(row_count // block_rows, dtype=jnp.int32) * block_rows
    mixed, log_sums = lax.map(one_block, starts)
    return (mixed.reshape(row_count, query.shape[1], query.shape[2]), log_sums)


def attention_backward(query, keys, values, log_sums, grad_mixed, length, block_rows):
    row_count = keys.shape[0]

    def one_block(carry, inputs):
        grad_keys, grad_values = carry
        start, block_sums = inputs
        block_query = lax.dynamic_slice_in_dim(query, start, block_rows, 0)
        block_grad = lax.dynamic_slice_in_dim(grad_mixed, start, block_rows, 0)
        scores = block_scores(block_query, keys, start, block_rows, length)
        probs = jnp.exp(scores - block_sums[..., None])
        grad_probs = jnp.einsum(
            "qhd,kd->hqk", block_grad, values, preferred_element_type=jnp.float32
        )
        inner = jnp.sum(probs * grad_probs, axis=-1, keepdims=True)
        grad_scores = (probs * (grad_probs - inner)).astype(jnp.bfloat16)
        grad_query = (
            jnp.einsum("hqk,kd->qhd", grad_scores, keys, preferred_element_type=jnp.float32)
            * 0.0625
        )
        grad_keys = (
            grad_keys
            + jnp.einsum(
                "hqk,qhd->kd", grad_scores, block_query, preferred_element_type=jnp.float32
            )
            * 0.0625
        )
        grad_values = grad_values + jnp.einsum(
            "hqk,qhd->kd",
            probs.astype(jnp.bfloat16),
            block_grad,
            preferred_element_type=jnp.float32,
        )
        return ((grad_keys, grad_values), grad_query)

    starts = jnp.arange(row_count // block_rows, dtype=jnp.int32) * block_rows
    zeros_keys = jnp.zeros((row_count, keys.shape[1]), jnp.float32)
    (grad_keys, grad_values), grad_query = lax.scan(
        one_block, (zeros_keys, zeros_keys), (starts, log_sums)
    )
    return (grad_query.reshape(row_count, query.shape[1], query.shape[2]), grad_keys, grad_values)


def local(
    tokens,
    cotangent,
    lengths,
    rates,
    query_weight,
    query_moment,
    query_average,
    output_weight,
    output_moment,
    output_average,
    gating_weight,
    gating_moment,
    gating_average,
    down_weight,
    down_moment,
    down_average,
    context_weight,
    context_moment,
    context_average,
    gains_weight,
    gains_moment,
    gains_average,
):
    row_count = tokens.shape[0]
    own_count = row_count // lax.axis_size("mp")
    own_start = lax.axis_index("mp") * own_count
    block_rows = 512
    length = lengths[0]
    inputs = tokens.astype(jnp.float32)
    places = jnp.arange(row_count, dtype=jnp.int32)
    valid = (places < length).astype(jnp.float32)[:, None]

    def own_rows(tensor):
        return lax.dynamic_slice_in_dim(tensor, own_start, own_count, 0)

    w_query, w_output, w_gating, w_down = (
        lax.all_gather(query_weight.astype(jnp.bfloat16), "dp", axis=0, tiled=True),
        lax.all_gather(output_weight.astype(jnp.bfloat16), "dp", axis=1, tiled=True),
        lax.all_gather(gating_weight.astype(jnp.bfloat16), "dp", axis=1, tiled=True),
        lax.all_gather(down_weight.astype(jnp.bfloat16), "dp", axis=1, tiled=True),
    )
    w_context, gains = (
        lax.all_gather(context_weight, ("dp", "mp"), axis=1, tiled=True),
        lax.all_gather(gains_weight, ("dp", "mp"), axis=1, tiled=True),
    )
    w_context = w_context.astype(jnp.bfloat16)
    heads_here = w_query.shape[1] // HD
    cosine, sine_tab = rotation(row_count, HD)
    normed = rms_norm(inputs, gains[0]).astype(jnp.bfloat16)
    query_raw = jnp.dot(normed, w_query, preferred_element_type=jnp.float32).reshape(
        row_count, heads_here, HD
    )
    keys_raw = jnp.dot(normed, w_context[0], preferred_element_type=jnp.float32)
    values = jnp.dot(normed, w_context[1], preferred_element_type=jnp.float32).astype(jnp.bfloat16)
    query = rotate(query_raw, cosine, sine_tab).astype(jnp.bfloat16)
    keys = rotate(keys_raw[:, None, :], cosine, sine_tab)[:, 0].astype(jnp.bfloat16)
    mixed, log_sums = attention_forward(query, keys, values, length, block_rows)
    mixed = mixed.reshape(row_count, heads_here * HD).astype(jnp.bfloat16)
    branch_part = jnp.dot(mixed, w_output, preferred_element_type=jnp.float32)
    middle = own_rows(inputs) + lax.psum_scatter(branch_part, "mp", scatter_dimension=0, tiled=True)
    normed_two = lax.all_gather(
        rms_norm(middle, gains[1]).astype(jnp.bfloat16), "mp", axis=0, tiled=True
    )
    gate_pre = jnp.dot(normed_two, w_gating[0], preferred_element_type=jnp.float32)
    up_pre = jnp.dot(normed_two, w_gating[1], preferred_element_type=jnp.float32)
    hidden_full, unit_pull = jax.vjp(gated_unit, gate_pre, up_pre)
    hidden = hidden_full.astype(jnp.bfloat16)
    feed_part = jnp.dot(hidden, w_down, preferred_element_type=jnp.float32)
    grad_out = cotangent.astype(jnp.float32) * valid
    grad_low = grad_out.astype(jnp.bfloat16)
    d_down = jnp.dot(hidden.T, grad_low, preferred_element_type=jnp.float32)
    grad_gate, grad_up = unit_pull(jnp.dot(grad_low, w_down.T, preferred_element_type=jnp.float32))
    grad_gate = grad_gate.astype(jnp.bfloat16)
    grad_up = grad_up.astype(jnp.bfloat16)
    d_gating = jnp.stack(
        [
            jnp.dot(normed_two.T, grad_gate, preferred_element_type=jnp.float32),
            jnp.dot(normed_two.T, grad_up, preferred_element_type=jnp.float32),
        ]
    )
    normed_two_part = jnp.dot(
        grad_gate, w_gating[0].T, preferred_element_type=jnp.float32
    ) + jnp.dot(grad_up, w_gating[1].T, preferred_element_type=jnp.float32)
    block_out = middle + lax.psum_scatter(
        feed_part.astype(jnp.bfloat16), "mp", scatter_dimension=0, tiled=True
    ).astype(jnp.float32)
    grad_normed_two = lax.psum_scatter(normed_two_part, "mp", scatter_dimension=0, tiled=True)
    grad_middle_own = own_rows(grad_out) + norm_back(grad_normed_two, middle, gains[1])
    middle_low = lax.all_gather(grad_middle_own.astype(jnp.bfloat16), "mp", axis=0, tiled=True)
    gain_two = jnp.sum(grad_normed_two * normalize(middle), axis=0)
    d_output = jnp.dot(mixed.T, middle_low, preferred_element_type=jnp.float32)
    grad_mixed = (
        jnp.dot(middle_low, w_output.T, preferred_element_type=jnp.float32)
        .astype(jnp.bfloat16)
        .reshape(row_count, heads_here, HD)
    )
    grad_query_rot, grad_keys_rot, grad_values_part = attention_backward(
        query, keys, values, log_sums, grad_mixed, length, block_rows
    )
    grad_query = (
        rotate(grad_query_rot, cosine, -sine_tab)
        .astype(jnp.bfloat16)
        .reshape(row_count, heads_here * HD)
    )
    grad_keys_part = rotate(grad_keys_rot[:, None, :], cosine, -sine_tab)[:, 0]
    d_query = jnp.dot(normed.T, grad_query, preferred_element_type=jnp.float32)
    normed_part = jnp.dot(grad_query, w_query.T, preferred_element_type=jnp.float32)
    grad_normed_own, grad_keys_own, grad_values_own = (
        lax.psum_scatter(normed_part, "mp", scatter_dimension=0, tiled=True),
        lax.psum_scatter(grad_keys_part, "mp", scatter_dimension=0, tiled=True),
        lax.psum_scatter(grad_values_part, "mp", scatter_dimension=0, tiled=True),
    )
    keys_low = grad_keys_own.astype(jnp.bfloat16)
    values_low = grad_values_own.astype(jnp.bfloat16)
    grad_normed_own = (
        grad_normed_own
        + jnp.dot(keys_low, w_context[0].T, preferred_element_type=jnp.float32)
        + jnp.dot(values_low, w_context[1].T, preferred_element_type=jnp.float32)
    )
    input_own = own_rows(inputs)
    normed_own = own_rows(normed)
    tokens_grad = grad_middle_own + norm_back(grad_normed_own, input_own, gains[0])
    gain_one = jnp.sum(grad_normed_own * normalize(input_own), axis=0)
    d_context = jnp.stack(
        [
            jnp.dot(normed_own.T, keys_low, preferred_element_type=jnp.float32),
            jnp.dot(normed_own.T, values_low, preferred_element_type=jnp.float32),
        ]
    )
    d_gains = jnp.stack([gain_one, gain_two])
    sum_query, sum_output, sum_gating, sum_down = (
        lax.psum_scatter(d_query, "dp", scatter_dimension=0, tiled=True),
        lax.psum_scatter(d_output, "dp", scatter_dimension=1, tiled=True),
        lax.psum_scatter(d_gating, "dp", scatter_dimension=1, tiled=True),
        lax.psum_scatter(d_down, "dp", scatter_dimension=1, tiled=True),
    )
    sum_context, sum_gains = (
        lax.psum_scatter(d_context, ("dp", "mp"), scatter_dimension=1, tiled=True),
        lax.psum_scatter(d_gains, ("dp", "mp"), scatter_dimension=1, tiled=True),
    )
    query_grads, query_moments, query_averages, query_updated = advance(
        sum_query, query_moment, query_average, query_weight, rates[0]
    )
    output_grads, output_moments, output_averages, output_updated = advance(
        sum_output, output_moment, output_average, output_weight, rates[1]
    )
    gating_grads, gating_moments, gating_averages, gating_updated = advance(
        sum_gating, gating_moment, gating_average, gating_weight, rates[2]
    )
    down_grads, down_moments, down_averages, down_updated = advance(
        sum_down, down_moment, down_average, down_weight, rates[3]
    )
    context_grads, context_moments, context_averages, context_updated = advance(
        sum_context, context_moment, context_average, context_weight, rates[4]
    )
    gains_grads, gains_moments, gains_averages, gains_updated = advance(
        sum_gains, gains_moment, gains_average, gains_weight, rates[5]
    )
    return (
        block_out,
        tokens_grad,
        query_grads,
        query_moments,
        query_averages,
        query_updated,
        output_grads,
        output_moments,
        output_averages,
        output_updated,
        gating_grads,
        gating_moments,
        gating_averages,
        gating_updated,
        down_grads,
        down_moments,
        down_averages,
        down_updated,
        context_grads,
        context_moments,
        context_averages,
        context_updated,
        gains_grads,
        gains_moments,
        gains_averages,
        gains_updated,
    )


def solution(mesh):
    return jax.shard_map(
        local,
        mesh=mesh,
        in_specs=(
            P("dp", None),
            P("dp", None),
            P("dp"),
            P(),
            P("dp", "mp"),
            P("dp", "mp"),
            P("dp", "mp"),
            P("mp", "dp"),
            P("mp", "dp"),
            P("mp", "dp"),
            P(None, "dp", "mp"),
            P(None, "dp", "mp"),
            P(None, "dp", "mp"),
            P("mp", "dp"),
            P("mp", "dp"),
            P("mp", "dp"),
            P(None, ("dp", "mp"), None),
            P(None, ("dp", "mp"), None),
            P(None, ("dp", "mp"), None),
            P(None, ("dp", "mp")),
            P(None, ("dp", "mp")),
            P(None, ("dp", "mp")),
        ),
        out_specs=(
            P(("dp", "mp"), None),
            P(("dp", "mp"), None),
            P("dp", "mp"),
            P("dp", "mp"),
            P("dp", "mp"),
            P("dp", "mp"),
            P("mp", "dp"),
            P("mp", "dp"),
            P("mp", "dp"),
            P("mp", "dp"),
            P(None, "dp", "mp"),
            P(None, "dp", "mp"),
            P(None, "dp", "mp"),
            P(None, "dp", "mp"),
            P("mp", "dp"),
            P("mp", "dp"),
            P("mp", "dp"),
            P("mp", "dp"),
            P(None, ("dp", "mp"), None),
            P(None, ("dp", "mp"), None),
            P(None, ("dp", "mp"), None),
            P(None, ("dp", "mp"), None),
            P(None, ("dp", "mp")),
            P(None, ("dp", "mp")),
            P(None, ("dp", "mp")),
            P(None, ("dp", "mp")),
        ),
        check_vma=False,
    )
```

profile of v0, /device:TPU:0, one launch (start us, length us, event | category | flops | bytes accessed | tf_op | source)
XLA Modules:
  0.0 1078.8 jit_solution(1245627835993001043)
XLA Ops:
  9.9 70.1 %all-gather = f32[32,36,2]{1,2,0:T(2,128)S(1)} all-gather(f32[1,36,2]{1,2,0:T(2,128)} %bitcast.247), channel_id=1, replica_groups=mesh['dp'=8,'mp'=4] {'dp','mp'}, dimensions={0}, use_global_device_ids=true | all-gather | bytes 9504 | tf_op jit(solution)/shard_map/all_gather | solution.py:177
  82.2 9.0 all_gather.25
  91.2 11.0 %all_gather.27 = bf16[256,1152]{0,1:T(8,128)(2,1)} all-gather(bf16[256,144]{0,1:T(8,128)(2,1)S(1)} %convert_element_type.183), channel_id=1, replica_groups=mesh['dp'=8,'mp'=4] {'dp'}, dimensions={1}, use_global_device_ids=true | all-gather | bytes 663552 | tf_op jit(solution)/shard_map/all_gather | solution.py:171
  108.8 2.4 fusion.77
  111.7 11.5 %while.29 = (s32[]{:T(128)}, bf16[2,512,1,256]{3,1,2,0:T(8,128)(2,1)S(1)}, f32[2,1,512]{2,1,0:T(1,128)S(1)}, s32[2]{0:T(128)S(1)}, s32[]{:T(128)}, /*index=5*/bf...) while((s32[]{:T(128)}, ...), condition=%wide.region_4.5_spmd.clone, body=%wide.region_1.4_spmd.sunk.clone | while | flops 542114816 | bytes 8153239 | solution.py:87
  123.3 3.1 fusion.102
  126.5 2.8 convert_element_type.185
  129.4 2.4 convert_element_type.173
  131.9 77.3 %reduce-scatter.11.cloned.1.call-done = f32[256,1152]{1,0:T(8,128)} async-done(((f32[1024,1152]{1,0:T(8,128)}), f32[256,1152]{1,0:T(8,128)}) %reduce-scatter.11.cloned.1.call-update) | async-done | bytes 1179664 | tf_op jit(solution)/shard_map/reduce_scatter | solution.py:193
  209.1 2.5 multiply_reduce_fusion.6
  214.5 48.7 %all-gather.9.cloned.1.call-done = bf16[1024,1152]{1,0:T(8,128)(2,1)} async-done(((bf16[256,1152]{1,0:T(8,128)(2,1)}), bf16[1024,1152]{1,0:T(8,128)(2,1)}) %all-gather.9.cloned.1.call-update) | async-done | bytes 2359312 | tf_op jit(solution)/shard_map/all_gather | solution.py:194
  263.3 10.7 fusion.40
  274.0 7.0 fusion.41
  280.9 19.6 %all-gather.13.cloned.1.call-done = bf16[1728,1152]{0,1:T(8,128)(2,1)} async-done(((bf16[1728,144]{0,1:T(8,128)(2,1)}), bf16[1728,1152]{0,1:T(8,128)(2,1)}) %all-gather.13.cloned.1.call-update) | async-done | bytes 3981328 | tf_op jit(solution)/shard_map/all_gather | solution.py:173
  300.6 18.1 %multiply_convert_fusion = (bf16[1024,1728]{0,1:T(8,128)(2,1)S(1)}, bf16[1024,1728]{0,1:T(8,128)(2,1)S(1)}, bf16[1024,1728]{0,1:T(8,128)(2,1)}) fusion(f32[1024,1728]{0,1:T(8,128)} %fusion.40, f32[1024,1728]{0,1:T(8,128)} %fusion.41, bf16[1728,1152]{0,1:T(8,128)(2,1)} %all-gather.13.cloned.1.call-done, f32[1024]{0:T(1024)S(1)} %fusion.90, ...), kind=kOutput, calls=%fused_computation.63 | convolution fusion | flops 4126408704 | bytes 31117312 | tf_op jit(solution)/shard_map/dot_general | solution.py:205
  318.7 9.8 fusion.39
  328.5 9.1 convolution_add_fusion.1
  337.6 9.7 convolution_convert_fusion
  347.5 4.2 convert_multiply_fusion
  351.7 71.2 %reduce-scatter.15.cloned.1.call-done = f32[256,1152]{1,0:T(8,128)} async-done(((f32[1024,1152]{1,0:T(8,128)}), f32[256,1152]{1,0:T(8,128)}) %reduce-scatter.15.cloned.1.call-update) | async-done | bytes 1179664 | tf_op jit(solution)/shard_map/reduce_scatter | solution.py:220
  424.6 49.1 %reduce-scatter.13.cloned.1.call-done = bf16[256,1152]{1,0:T(8,128)(2,1)} async-done(((bf16[1024,1152]{1,0:T(8,128)(2,1)}), bf16[256,1152]{1,0:T(8,128)(2,1)}) %reduce-scatter.13.cloned.1.call-update) | async-done | bytes 589840 | tf_op jit(solution)/shard_map/reduce_scatter | solution.py:217
  473.7 3.4 fusion.97
  477.2 49.5 %all-gather.15.cloned.1.call-done = bf16[1024,1152]{1,0:T(8,128)(2,1)} async-done(((bf16[256,1152]{1,0:T(8,128)(2,1)}), bf16[1024,1152]{1,0:T(8,128)(2,1)}) %all-gather.15.cloned.1.call-update) | async-done | bytes 2359312 | tf_op jit(solution)/shard_map/all_gather | solution.py:222
  526.7 3.3 fusion.42
  530.0 29.0 %while.30 = (s32[]{:T(128)}, f32[1024,256]{1,0:T(8,128)}, f32[1024,256]{1,0:T(8,128)}, f32[2,512,1,256]{3,1,2,0:T(8,128)}, s32[2]{0:T(128)S(1)}, /*index=5*/s32[...) while((s32[]{:T(128)}, f32[1024,256]{1,0:T(8,128)}, ...), condition=%wide.region_12.13_spmd.clone.clone, body=%wide.region_10.12_spmd.clone.sunk.clone | while | flops 1349387264 | bytes 39862636 | solution.py:127
  537.7 2.5 fusion.193
  541.7 2.5 convolution_add_fusion.6
  551.9 2.9 fusion.193
  556.2 2.8 convolution_add_fusion.6
  561.1 3.1 fusion.70
  566.4 9.9 convolution_bitcast_fusion.1
  576.6 6.9 convolution_bitcast_fusion.2
  583.5 5.8 pad_maximum_fusion
  589.3 26.9 %copy.116 = f32[2,1152,1728]{2,0,1:T(2,128)} copy(f32[2,1152,1728]{1,2,0:T(8,128)} %pad_maximum_fusion) | data formatting | bytes 31850496 | tf_op jit(solution)/shard_map/stack | solution.py:208
  617.9 8.7 fusion.45
  630.2 4.2 fusion.103
  637.8 7.6 copy.119
  646.8 3.0 fusion.83
  653.0 213.5 %all-reduce.6.cloned.1.call-done = f32[2,1152,1728]{2,0,1:T(2,128)} async-done(((f32[2,1152,1728]{2,0,1:T(2,128)}), f32[2,1152,1728]{2,0,1:T(2,128)}) %all-reduce.6.cloned.1.call-update) | async-done | bytes 15925264
  866.5 2.4 constant_dynamic-slice_fusion.3
  869.0 6.1 add_multiply_fusion
  875.3 4.7 add_multiply_fusion.1
  880.0 2.5 add_multiply_fusion.3
  884.9 135.9 %all-reduce.8.cloned.1.call-done = f32[2,1152,256]{2,0,1:T(2,128)} async-done(((f32[2,1152,256]{2,0,1:T(2,128)}), f32[2,1152,256]{2,0,1:T(2,128)}) %all-reduce.8.cloned.1.call-update) | async-done | bytes 2359312
  1020.7 2.4 add_multiply_fusion.4
  1024.9 2.5 multiply_reduce_fusion.2
  1027.4 39.0 %all-reduce.2 = f32[2,1152]{1,0:T(2,128)S(1)} all-reduce(f32[2,1152]{1,0:T(2,128)S(1)} %pad_maximum_fusion.6), channel_id=13, replica_groups=mesh['dp'=8,'mp'=4] {'dp','mp'}, use_global_device_ids=true, to_apply=%region_25.26.clone | all-reduce | flops 2304 | bytes 18432
  1067.1 2.6 fusion.44
  (248 shorter events, 60.0 us)
Async XLA Ops:
  8.0 94.1 %copy-start.3 = (bf16[1024,1152]{1,0:T(8,128)(2,1)S(1)}, bf16[1024,1152]{1,0:T(8,128)(2,1)}, u32[]{:S(2)}) copy-start(bf16[1024,1152]{1,0:T(8,128)(2,1)} %param.26) | copy-start | bytes 7077892
  8.0 97.2 %all-gather.7.cloned.1.call-start = ((), (), s32[]{:S(2)}) async-start(), calls=%async_computation.9 | async-start | bytes 1216512 | tf_op jit(solution)/shard_map/all_gather | solution.py:176
  9.8 199.3 %reduce-scatter.11.cloned.1.call-start = ((), (), s32[]{:S(2)}) async-start(), calls=%async_computation.10 | async-start | bytes 5898240 | tf_op jit(solution)/shard_map/reduce_scatter | solution.py:193
  81.0 21.7 %copy-start.4 = (bf16[1024,1152]{1,0:T(8,128)(2,1)S(1)}, bf16[1024,1152]{1,0:T(8,128)(2,1)}, u32[]{:S(2)}) copy-start(bf16[1024,1152]{1,0:T(8,128)(2,1)} %param.26) | copy-start | bytes 7077892
  82.1 21.2 %copy-start.43 = (f32[1152]{0:T(1024)}, f32[1152]{0:T(1024)S(1)}, u32[]{:S(2)}) copy-start(f32[1152]{0:T(1024)S(1)} %get-tuple-element.354) | copy-start | bytes 13828
  91.2 12.1 %copy-start.15 = (bf16[1152,256]{1,0:T(8,128)(2,1)}, bf16[1152,256]{1,0:T(8,128)(2,1)S(1)}, u32[]{:S(2)}) copy-start(bf16[1152,256]{1,0:T(8,128)(2,1)S(1)} %all_gather.25) | copy-start | bytes 1769476
  111.7 11.6 %copy-start.22 = (bf16[256,1152]{0,1:T(8,128)(2,1)S(1)}, bf16[256,1152]{0,1:T(8,128)(2,1)}, u32[]{:S(2)}) copy-start(bf16[256,1152]{0,1:T(8,128)(2,1)} %all_gather.27) | copy-start | bytes 1769476
  126.5 88.0 %all-gather.11.cloned.1.call-start = ((), (), s32[]{:S(2)}) async-start(), calls=%async_computation.12 | async-start | bytes 9289728 | tf_op jit(solution)/shard_map/all_gather | solution.py:172
  129.3 133.9 %all-gather.9.cloned.1.call-start = ((), (), s32[]{:S(2)}) async-start(), calls=%async_computation.11 | async-start | bytes 2949120 | tf_op jit(solution)/shard_map/all_gather | solution.py:194
  131.8 80.8 %copy-start.20 = (f32[1728,144]{0,1:T(8,128)S(1)}, f32[1728,144]{0,1:T(8,128)}, u32[]{:S(2)}) copy-start(f32[1728,144]{0,1:T(8,128)} %param.39) | copy-start | bytes 2985988
  212.6 87.9 %all-gather.13.cloned.1.call-start = ((), (), s32[]{:S(2)}) async-start(), calls=%async_computation.13 | async-start | bytes 4644864 | tf_op jit(solution)/shard_map/all_gather | solution.py:173
  213.6 209.4 %reduce-scatter.15.cloned.1.call-start = ((), (), s32[]{:S(2)}) async-start(), calls=%async_computation.15 | async-start | bytes 5898240 | tf_op jit(solution)/shard_map/reduce_scatter | solution.py:220
  263.3 10.7 copy-start.51
  263.3 10.7 copy-start.52
  318.7 9.8 copy-start.56
  318.7 9.8 copy-start.55
  337.6 136.2 %reduce-scatter.13.cloned.1.call-start = ((), (), s32[]{:S(2)}) async-start(), calls=%async_computation.14 | async-start | bytes 2949120 | tf_op jit(solution)/shard_map/reduce_scatter | solution.py:217
  347.3 179.4 %all-gather.15.cloned.1.call-start = ((), (), s32[]{:S(2)}) async-start(), calls=%async_computation.16 | async-start | bytes 2949120 | tf_op jit(solution)/shard_map/all_gather | solution.py:222
  423.0 50.8 %copy-start.17 = (f32[256,1152]{1,0:T(8,128)S(1)}, f32[256,1152]{1,0:T(8,128)}, u32[]{:S(2)}) copy-start(f32[256,1152]{1,0:T(8,128)} %reduce-scatter.15.cloned.1.call-done) | copy-start | bytes 3538948
  424.6 102.1 %copy-start.23 = (bf16[256,1152]{0,1:T(8,128)(2,1)S(1)}, bf16[256,1152]{0,1:T(8,128)(2,1)}, u32[]{:S(2)}) copy-start(bf16[256,1152]{0,1:T(8,128)(2,1)} %all_gather.27) | copy-start | bytes 1769476
  477.1 157.7 %reduce-scatter.19.cloned.1.call-start = ((), (), s32[]{:S(2)}) async-start(), calls=%async_computation.18 | async-start | bytes 1310720 | tf_op jit(solution)/shard_map/reduce_scatter | solution.py:243
  530.0 7.4 copy-start.6
  530.0 5.3 copy-start.36
  544.2 7.4 copy-start.6
  544.2 5.3 copy-start.36
  564.2 62.5 %copy-start.27 = (bf16[1024,128]{0,1:T(8,128)(2,1)}, bf16[1024,128]{0,1:T(8,128)(2,1)S(1)}, u32[]{:S(2)}) copy-start(bf16[1024,128]{0,1:T(8,128)(2,1)S(1)} %get-tuple-element.437) | copy-start | bytes 786436
  565.3 70.9 %reduce-scatter.21.cloned.1.call-start = ((), (), s32[]{:S(2)}) async-start(), calls=%async_computation.19 | async-start | bytes 1310720 | tf_op jit(solution)/shard_map/reduce_scatter | solution.py:244
  576.3 290.2 %all-reduce.6.cloned.1.call-start = ((), (), s32[]{:S(2)}) async-start(), calls=%async_computation.23 | async-start | bytes 33030144
  576.6 7.0 copy-start.9
  616.2 258.9 %reduce-scatter.27.cloned.1.call-start = ((), (), s32[]{:S(2)}) async-start(), calls=%async_computation.22 | async-start | bytes 9289728 | tf_op jit(solution)/shard_map/reduce_scatter | solution.py:268
  626.7 253.3 %reduce-scatter.23.cloned.1.call-start = ((), (), s32[]{:S(2)}) async-start(), calls=%async_computation.20 | async-start | bytes 1327104 | tf_op jit(solution)/shard_map/reduce_scatter | solution.py:265
  630.2 252.3 %reduce-scatter.25.cloned.1.call-start = ((), (), s32[]{:S(2)}) async-start(), calls=%async_computation.21 | async-start | bytes 1327104 | tf_op jit(solution)/shard_map/reduce_scatter | solution.py:266
  634.5 386.2 %all-reduce.8.cloned.1.call-start = ((), (), s32[]{:S(2)}) async-start(), calls=%async_computation.24 | async-start | bytes 4718592
  645.5 377.7 %reduce-scatter.17.cloned.1.call-start = ((), (), s32[]{:S(2)}) async-start(), calls=%async_computation.17 | async-start | bytes 5898240 | tf_op jit(solution)/shard_map/reduce_scatter | solution.py:242
  649.8 219.2 %copy-start.8 = (f32[2,144,1728]{2,1,0:T(8,128)S(1)}, f32[2,144,1728]{2,1,0:T(8,128)}, u32[]{:S(2)}) copy-start(f32[2,144,1728]{2,1,0:T(8,128)} %param.36) | copy-start | bytes 5971972
  869.0 6.2 copy-start.21
  875.2 4.8 copy-start.33
  875.2 4.8 copy-start.39
  875.2 4.8 copy-start.40
  875.2 7.3 copy-start.34
  875.2 7.3 copy-start.41
  875.2 7.3 copy-start.42
  875.2 145.5 %copy-start.38 = (f32[2,36,256]{2,0,1:T(2,128)S(1)}, f32[2,36,256]{2,0,1:T(2,128)}, u32[]{:S(2)}) copy-start(f32[2,36,256]{2,0,1:T(2,128)} %param.42) | copy-start | bytes 221188
  875.3 145.5 %copy-start.45 = (f32[2,36,256]{2,0,1:T(2,128)S(1)}, f32[2,36,256]{2,0,1:T(2,128)}, u32[]{:S(2)}) copy-start(f32[2,36,256]{2,0,1:T(2,128)} %param.44) | copy-start | bytes 221188
  880.0 143.2 %copy-start.13 = (bf16[2,1152,256]{2,1,0:T(8,128)(2,1)S(1)}, bf16[2,1152,256]{2,1,0:T(8,128)(2,1)}, u32[]{:S(2)}) copy-start(bf16[2,1152,256]{2,1,0:T(8,128)(2,1)} %copy-done.12) | copy-start | bytes 3538948
  880.0 143.2 %copy-start.26 = (f32[256,256]{0,1:T(8,128)S(1)}, f32[256,256]{0,1:T(8,128)}, u32[]{:S(2)}) copy-start(f32[256,256]{0,1:T(8,128)} %reduce-scatter.19.cloned.1.call-done) | copy-start | bytes 786436
  882.5 142.3 %copy-start.44 = (f32[1152]{0:T(1024)S(1)}, f32[1152]{0:T(1024)}, u32[]{:S(2)}) copy-start(f32[1152]{0:T(1024)} %copy-done.43) | copy-start | bytes 13828
  1024.8 42.2 %copy-start.18 = (f32[256,1152]{1,0:T(8,128)S(1)}, f32[256,1152]{1,0:T(8,128)}, u32[]{:S(2)}) copy-start(f32[256,1152]{1,0:T(8,128)} %get-tuple-element.415) | copy-start | bytes 3538948
  (31 other events, 68.2 us)
Sparse Core Ops, SparseCore 0:
  12.3 56.7 all-gather.6
  126.6 82.5 reduce-scatter.10
  337.7 85.2 reduce-scatter.14
  425.1 48.5 reduce-scatter.12
  565.4 25.7 reduce-scatter.18
  594.1 25.7 reduce-scatter.20
  626.8 84.1 reduce-scatter.26
  715.1 46.9 reduce-scatter.22
  765.9 40.7 reduce-scatter.24
  808.9 85.4 reduce-scatter.16
Sparse Core Ops, SparseCore 1:
  129.4 50.9 all-gather.10
  212.7 50.5 all-gather.8
  265.6 34.9 all-gather.12
  477.2 49.5 all-gather.14
  616.3 250.2 all-reduce.5
  872.1 148.6 all-reduce.7
where the time goes:
time: 1090 us; the launch traced here: 1080 us
  waiting for transfers between devices  665 us (61%)
  matrix products  137 us (13%)
  blocking collectives  129 us (12%)
  other arithmetic  66.2 us (6%)
  local copies, waits for them, and re-layouts  53.4 us (5%)
  between operations  18.3 us (2%)
    unnamed x18, waiting for transfers between devices  350 us
    reduce_scatter x1, waiting for transfers between devices, local(): lax.psum_scatter(branch_part, 'mp', scatter_dimension=0, tiled=True)  77.3 us
    reduce_scatter x1, waiting for transfers between devices, local(): lax.psum_scatter(normed_two_part, 'mp', scatter_dimension=0, tiled=True)  71.2 us
    all_gather x1, blocking collectives, local(): lax.all_gather(gains_weight, ('dp', 'mp'), axis=1, tiled=True)  70.1 us
    all_gather x1, waiting for transfers between devices, local(): lax.all_gather(grad_middle_own.astype(jnp.bfloat16), 'mp', axis=0, tiled=...  49.5 us
    reduce_scatter x1, waiting for transfers between devices, local(): lax.psum_scatter(feed_part.astype(jnp.bfloat16), 'mp', scatter_dimension=...  49.1 us
    all_gather x1, waiting for transfers between devices, local(): lax.all_gather(rms_norm(middle, gains[1]).astype(jnp.bfloat16), 'mp', axi...  48.7 us
    unnamed x1, blocking collectives  39 us
  transfers between devices with their start and end apart: 16, of which 8 were waited for; matrix products, arithmetic and copies ran while one was open for 14% of the time, Pallas kernels for 0%

commit v1 on v0

v1 whole, which is shorter than its diff:
```python
import jax
import jax.numpy as jnp
from jax import lax
from jax.sharding import PartitionSpec as P

HD = 256
LANES = 128
EPSILON = 1e-06
MOMENTUM = 0.9
AVERAGING = 0.5
BF = jnp.bfloat16
F32 = jnp.float32


def mm(a, b, dims):
    return lax.dot_general(a, b, (dims, ((), ())), preferred_element_type=F32)


def inverse_rms(tensor):
    return lax.rsqrt(jnp.mean(tensor * tensor, axis=-1, keepdims=True) + EPSILON)


def norm_back(grad_in, unit, inverse, gain_vec):
    scaled = grad_in * gain_vec
    return inverse * (scaled - unit * jnp.mean(scaled * unit, axis=-1, keepdims=True))


def rotation(length, head_size):
    halfway = head_size // 2
    frequency = 1000000.0 ** (-(jnp.arange(halfway).astype(F32) * 2.0 / head_size))
    angles = jnp.arange(length).astype(F32)[:, None] * frequency[None, :]
    return (jnp.cos(angles), jnp.sin(angles))


def rotate(tensor, cosine, sine_tab):
    halfway = tensor.shape[-1] // 2
    former = tensor[..., :halfway]
    latter = tensor[..., halfway:]
    return jnp.concatenate(
        [former * cosine - latter * sine_tab, latter * cosine + former * sine_tab], axis=-1
    )


def advance(gradient, moment, average, weight, step_rate):
    moment_new = MOMENTUM * moment + gradient
    weight_new = weight - step_rate * (gradient + MOMENTUM * moment_new)
    average_new = AVERAGING * average + (1.0 - AVERAGING) * weight_new
    return (gradient, moment_new, average_new, weight_new)


def swap(tensor, bit):
    count = lax.axis_size("dp")
    return lax.ppermute(tensor, "dp", [(i, i ^ bit) for i in range(count)])


def from_behind(tensor, step):
    count = lax.axis_size("mp")
    return lax.ppermute(tensor, "mp", [(i, (i + step) % count) for i in range(count)])


def from_ahead(tensor, step):
    count = lax.axis_size("mp")
    return lax.ppermute(tensor, "mp", [(i, (i - step) % count) for i in range(count)])


def bit_orders():
    bits = []
    while 2 ** len(bits) < lax.axis_size("dp"):
        bits.append(2 ** len(bits))
    outer = bits[1:]
    return (outer + bits[:1], outer[::-1] + bits[:1])


def spread(tensor, order):
    held = {0: tensor}
    for bit in order:
        held.update({k ^ bit: swap(piece, bit) for k, piece in list(held.items())})
    return held


def assemble(flows):
    me = lax.axis_index("dp")
    count = lax.axis_size("dp")
    share = flows[0][0].shape[0]
    width = sum(held[0].shape[1] for held in flows)
    whole = jnp.zeros((count * share, width), flows[0][0].dtype)
    column = 0
    for held in flows:
        for k in sorted(held):
            whole = lax.dynamic_update_slice(whole, held[k], ((me ^ k) * share, column))
        column += held[0].shape[1]
    return whole


def collect(tensor, order):
    me = lax.axis_index("dp")
    count = lax.axis_size("dp")
    depth = len(order)
    current = tensor.reshape((2,) * depth + (tensor.shape[0] // count, tensor.shape[1]))
    left = [2**j for j in reversed(range(depth))]
    for n, bit in enumerate(order):
        axis = left.index(bit)
        side = (me // bit) % 2
        keep = lax.dynamic_index_in_dim(current, side, axis, keepdims=False)
        send = lax.dynamic_index_in_dim(current, 1 - side, axis, keepdims=False)
        left.remove(bit)
        current = keep.astype(F32) + swap(send, bit).astype(F32)
        if n < depth - 1:
            current = current.astype(BF)
    return current


def split_three(tensor):
    high = lax.reduce_precision(tensor, 8, 7)
    rest = tensor - high
    middle = lax.reduce_precision(rest, 8, 7)
    return [high.astype(BF), middle.astype(BF), (rest - middle).astype(BF)]


def halves(tensor):
    cut = -(-tensor.shape[1] // (2 * LANES)) * LANES
    return (tensor[:, :cut], tensor[:, cut:])


def local(
    tokens,
    cotangent,
    lengths,
    rates,
    query_weight,
    query_moment,
    query_average,
    output_weight,
    output_moment,
    output_average,
    gating_weight,
    gating_moment,
    gating_average,
    down_weight,
    down_moment,
    down_average,
    context_weight,
    context_moment,
    context_average,
    gains_weight,
    gains_moment,
    gains_average,
):
    row_count, width = tokens.shape
    dp, mp = lax.axis_size("dp"), lax.axis_size("mp")
    place = lax.axis_index("mp")
    own_count = row_count // mp
    own_start = place * own_count
    share, piece = width // dp, width // (dp * mp)
    forth, back = bit_orders()
    forth_first, back_first = forth[-1:] + forth[:-1], back[-1:] + back[:-1]
    length = lengths[0]
    inputs = tokens.astype(F32)
    places = jnp.arange(row_count, dtype=jnp.int32)
    valid = (places < length).astype(F32)[:, None]

    def own_rows(tensor):
        return lax.dynamic_slice_in_dim(tensor, own_start, own_count, 0)

    def rows_at(tensor, step, count):
        return lax.dynamic_slice_in_dim(tensor, ((place - step) % mp) * count, count, 0)

    def gather_heads(tensor):
        return jnp.concatenate([tensor] + [from_behind(tensor, k) for k in range(1, mp)], axis=1)

    w_context_own = context_weight.astype(BF)
    gains_split = split_three(gains_weight)
    context_own = jnp.concatenate(
        [w_context_own[0], w_context_own[1]]
        + [part.T for part in gains_split]
        + [jnp.zeros((piece, LANES - 2 * len(gains_split)), BF)],
        axis=1,
    )
    context_parts = [context_own] + [from_behind(context_own, k) for k in range(1, mp)]
    ring = context_parts[::-1] * 2
    context_share = lax.dynamic_slice_in_dim(
        jnp.concatenate(ring, axis=0), (mp - 1 - place) * piece, share, 0
    )
    context_full = assemble([spread(context_share, back)])
    query_share = gather_heads(query_weight.astype(BF))
    w_query = assemble([spread(query_share, forth)])
    output_share = gather_heads(output_weight.T.astype(BF))
    output_a, output_b = halves(output_share)
    w_output = assemble([spread(output_a, forth), spread(output_b, back)])
    gating_low = gating_weight.astype(BF)
    down_a, down_b = halves(down_weight.T.astype(BF))
    w_gate = assemble([spread(gating_low[0], forth)])
    w_up = assemble([spread(gating_low[1], back)])
    w_down = assemble([spread(down_a, forth), spread(down_b, back)])

    w_context = context_full[:, : 2 * HD]
    gain_terms = context_full[:, 2 * HD : 2 * HD + 6].astype(F32).T
    gains = gain_terms[0:2] + gain_terms[2:4] + gain_terms[4:6]

    cosine, sine_tab = rotation(row_count, HD)
    cosine_own, sine_own = own_rows(cosine), own_rows(sine_tab)
    inverse = inverse_rms(inputs)
    normed = (inputs * inverse * gains[0]).astype(BF)
    normed_own = own_rows(normed)
    context_raw = mm(normed, w_context, ((1,), (0,)))
    keys = rotate(context_raw[:, :HD], cosine, sine_tab).astype(BF)
    values = context_raw[:, HD:].astype(BF)
    query_raw = mm(normed_own, w_query, ((1,), (0,)))
    heads = query_raw.shape[1] // HD
    query_heads = [
        rotate(query_raw[:, h * HD : (h + 1) * HD], cosine_own, sine_own).astype(BF)
        for h in range(heads)
    ]
    query = jnp.stack(query_heads)
    scores = jnp.einsum("hqd,kd->hqk", query, keys, preferred_element_type=F32) * 0.0625
    rows_here = own_start + jnp.arange(own_count, dtype=jnp.int32)
    allowed = (places[None, :] <= rows_here[:, None]) & (places[None, :] < length)
    scores = jnp.where(allowed[None], scores, -1e30)
    exped = jnp.exp(scores - jnp.max(scores, axis=-1, keepdims=True))
    probs = exped / jnp.sum(exped, axis=-1, keepdims=True)
    probs_low = probs.astype(BF)
    mixed_heads = jnp.einsum("hqk,kd->hqd", probs_low, values, preferred_element_type=F32)
    mixed = jnp.concatenate([mixed_heads[h].astype(BF) for h in range(heads)], axis=1)
    input_own = own_rows(inputs)
    middle = input_own + mm(mixed, w_output, ((1,), (1,)))
    inverse_two = inverse_rms(middle)
    unit_two = middle * inverse_two
    normed_two_own = (unit_two * gains[1]).astype(BF)

    normed_two = jnp.concatenate(
        [normed_two_own] + [from_behind(normed_two_own, k) for k in range(1, mp)], axis=0
    )
    grad_out = cotangent.astype(F32) * valid
    grad_low = grad_out.astype(BF)
    grad_rows = jnp.concatenate([rows_at(grad_low, k, own_count) for k in range(mp)], axis=0)
    gate_pre = mm(normed_two, w_gate, ((1,), (0,)))
    up_pre = mm(normed_two, w_up, ((1,), (0,)))
    grad_hidden = mm(grad_rows, w_down, ((1,), (0,)))

    def gated_unit(gate, up):
        return jax.nn.gelu(gate, approximate=True) * up

    hidden_full, unit_pull = jax.vjp(gated_unit, gate_pre, up_pre)
    hidden = hidden_full.astype(BF)
    grad_gate, grad_up = (part.astype(BF) for part in unit_pull(grad_hidden))
    normed_two_part = mm(grad_gate, w_gate, ((1,), (1,))) + mm(grad_up, w_up, ((1,), (1,)))

    def to_owners(part):
        total = part[:own_count]
        for k in range(1, mp):
            sent = from_ahead(part[k * own_count : (k + 1) * own_count].astype(BF), k)
            total = total + sent.astype(F32)
        return total

    grad_normed_two = to_owners(normed_two_part)
    feed_part = mm(hidden, w_down, ((1,), (1,)))
    block_out = middle + to_owners(feed_part)
    d_gate = mm(normed_two, grad_gate, ((0,), (0,))).astype(BF)
    d_up = mm(normed_two, grad_up, ((0,), (0,))).astype(BF)
    d_down = mm(grad_rows, hidden, ((0,), (0,))).astype(BF)

    grad_middle = own_rows(grad_out) + norm_back(grad_normed_two, unit_two, inverse_two, gains[1])
    middle_low = grad_middle.astype(BF)
    gain_two = jnp.sum(grad_normed_two * unit_two, axis=0)
    d_output = mm(middle_low, mixed, ((0,), (0,))).astype(BF)
    grad_mixed = mm(middle_low, w_output, ((1,), (0,))).astype(BF)
    grad_heads = jnp.stack([grad_mixed[:, h * HD : (h + 1) * HD] for h in range(heads)])
    grad_probs = jnp.einsum("hqd,kd->hqk", grad_heads, values, preferred_element_type=F32)
    inner = jnp.sum(probs * grad_probs, axis=-1, keepdims=True)
    grad_scores = (probs * (grad_probs - inner)).astype(BF)
    grad_query_rot = jnp.einsum("hqk,kd->hqd", grad_scores, keys, preferred_element_type=F32)
    grad_keys_rot = jnp.einsum("hqk,hqd->kd", grad_scores, query, preferred_element_type=F32)
    grad_values = jnp.einsum("hqk,hqd->kd", probs_low, grad_heads, preferred_element_type=F32)
    grad_query = jnp.concatenate(
        [
            rotate(grad_query_rot[h] * 0.0625, cosine_own, -sine_own).astype(BF)
            for h in range(heads)
        ],
        axis=1,
    )
    grad_keys = rotate(grad_keys_rot * 0.0625, cosine, -sine_tab)
    grad_context = jnp.concatenate([grad_keys.astype(BF), grad_values.astype(BF)], axis=1)

    grad_context_own = rows_at(grad_context, 0, own_count).astype(F32)
    for k in range(1, mp):
        sent = from_ahead(rows_at(grad_context, k, own_count), k)
        grad_context_own = grad_context_own + sent.astype(F32)
    grad_normed = mm(grad_query, w_query, ((1,), (1,))) + mm(
        grad_context_own.astype(BF), w_context, ((1,), (1,))
    )
    inverse_own = own_rows(inverse)
    tokens_grad = grad_middle + norm_back(
        grad_normed, input_own * inverse_own, inverse_own, gains[0]
    )

    d_query = mm(normed_own, grad_query, ((0,), (0,)))
    d_context = mm(normed, grad_context, ((0,), (0,)))
    gain_one = (
        jnp.sum(d_query * w_query.astype(F32), axis=1)
        + jnp.sum(d_context * w_context.astype(F32), axis=1)
    ) / gains[0]
    d_context = jnp.concatenate(
        [
            d_context.astype(BF),
            gain_one[:, None].astype(BF),
            gain_two[:, None].astype(BF),
            jnp.zeros((width, LANES - 2), BF),
        ],
        axis=1,
    )

    def join(parts):
        return jnp.concatenate(parts, axis=1)

    d_down_a, d_down_b = halves(d_down)
    d_output_a, d_output_b = halves(d_output)
    sum_gate = collect(d_gate, forth_first)
    sum_up = collect(d_up, back_first)
    sum_down = join([collect(d_down_a, forth_first), collect(d_down_b, back_first)]).T
    share_output = join([collect(d_output_a, forth_first), collect(d_output_b, back_first)])
    share_query = collect(d_query.astype(BF), forth_first)
    share_context = collect(d_context, back_first)

    def heads_to_owners(part):
        total = part[:, :HD]
        for k in range(1, mp):
            sent = from_ahead(part[:, k * HD : (k + 1) * HD].astype(BF), k)
            total = total + sent.astype(F32)
        return total

    sum_output = heads_to_owners(share_output).T
    sum_query = heads_to_owners(share_query)
    sum_context = rows_at(share_context, 0, piece)
    for k in range(1, mp):
        sent = from_ahead(rows_at(share_context, k, piece).astype(BF), k)
        sum_context = sum_context + sent.astype(F32)
    sum_gains = sum_context[:, 2 * HD : 2 * HD + 2].T
    sum_context = jnp.stack([sum_context[:, :HD], sum_context[:, HD : 2 * HD]])
    sum_gating = jnp.stack([sum_gate, sum_up])

    query_grads, query_moments, query_averages, query_updated = advance(
        sum_query, query_moment, query_average, query_weight, rates[0]
    )
    output_grads, output_moments, output_averages, output_updated = advance(
        sum_output, output_moment, output_average, output_weight, rates[1]
    )
    gating_grads, gating_moments, gating_averages, gating_updated = advance(
        sum_gating, gating_moment, gating_average, gating_weight, rates[2]
    )
    down_grads, down_moments, down_averages, down_updated = advance(
        sum_down, down_moment, down_average, down_weight, rates[3]
    )
    context_grads, context_moments, context_averages, context_updated = advance(
        sum_context, context_moment, context_average, context_weight, rates[4]
    )
    gains_grads, gains_moments, gains_averages, gains_updated = advance(
        sum_gains, gains_moment, gains_average, gains_weight, rates[5]
    )
    return (
        block_out,
        tokens_grad,
        query_grads,
        query_moments,
        query_averages,
        query_updated,
        output_grads,
        output_moments,
        output_averages,
        output_updated,
        gating_grads,
        gating_moments,
        gating_averages,
        gating_updated,
        down_grads,
        down_moments,
        down_averages,
        down_updated,
        context_grads,
        context_moments,
        context_averages,
        context_updated,
        gains_grads,
        gains_moments,
        gains_averages,
        gains_updated,
    )


def solution(mesh):
    return jax.shard_map(
        local,
        mesh=mesh,
        in_specs=(
            P("dp", None),
            P("dp", None),
            P("dp"),
            P(),
            P("dp", "mp"),
            P("dp", "mp"),
            P("dp", "mp"),
            P("mp", "dp"),
            P("mp", "dp"),
            P("mp", "dp"),
            P(None, "dp", "mp"),
            P(None, "dp", "mp"),
            P(None, "dp", "mp"),
            P("mp", "dp"),
            P("mp", "dp"),
            P("mp", "dp"),
            P(None, ("dp", "mp"), None),
            P(None, ("dp", "mp"), None),
            P(None, ("dp", "mp"), None),
            P(None, ("dp", "mp")),
            P(None, ("dp", "mp")),
            P(None, ("dp", "mp")),
        ),
        out_specs=(
            P(("dp", "mp"), None),
            P(("dp", "mp"), None),
            P("dp", "mp"),
            P("dp", "mp"),
            P("dp", "mp"),
            P("dp", "mp"),
            P("mp", "dp"),
            P("mp", "dp"),
            P("mp", "dp"),
            P("mp", "dp"),
            P(None, "dp", "mp"),
            P(None, "dp", "mp"),
            P(None, "dp", "mp"),
            P(None, "dp", "mp"),
            P("mp", "dp"),
            P("mp", "dp"),
            P("mp", "dp"),
            P("mp", "dp"),
            P(None, ("dp", "mp"), None),
            P(None, ("dp", "mp"), None),
            P(None, ("dp", "mp"), None),
            P(None, ("dp", "mp"), None),
            P(None, ("dp", "mp")),
            P(None, ("dp", "mp")),
            P(None, ("dp", "mp")),
            P(None, ("dp", "mp")),
        ),
        check_vma=False,
    )
```

time: 1090 us -> 631 us (0.58)
  waiting for transfers between devices: 665 us -> 193 us
  blocking collectives: 129 us -> 0 us
  starting transfers between devices: 1.52 us -> 113 us
  local copies, waits for them, and re-layouts: 53.4 us -> 132 us
  matrix products: 137 us -> 113 us
  between operations: 18.3 us -> 3.9 us
    unnamed x18 -> x0, waiting for transfers between devices: 350 us -> none
    reduce_scatter x9 -> x0, waiting for transfers between devices: 198 us -> none  [the longest x1 77.3 us: local(): lax.psum_scatter(branch_part, 'mp', scatter_dimension=0, tiled=True)]
    ppermute x0 -> x110, waiting for transfers between devices: none -> 193 us  [the longest x80 126 us: swap(): return lax.ppermute(tensor, 'dp', [(i, i ^ bit) for i in range(count)])]
    all_gather x5 -> x0, waiting for transfers between devices: 118 us -> none  [the longest x1 49.5 us: local(): lax.all_gather(grad_middle_own.astype(jnp.bfloat16), 'mp', axis=0, tiled=...]
    ppermute x0 -> x110, starting transfers between devices: none -> 113 us  [the longest x80 54.4 us: swap(): return lax.ppermute(tensor, 'dp', [(i, i ^ bit) for i in range(count)])]
    all_gather x3 -> x0, blocking collectives: 90 us -> none  [the longest x1 70.1 us: local(): lax.all_gather(gains_weight, ('dp', 'mp'), axis=1, tiled=True)]
    unnamed x1 -> x0, blocking collectives: 39 us -> none
    dynamic_update_slice x2 -> x60, local copies, waits for them, and re-layouts: 0.02 us -> 26.4 us  [assemble(): whole = lax.dynamic_update_slice(whole, held[k], ((me ^ k) * share, column))]
  transfers between devices with their start and end apart: 16 -> 110, of which waited for: 8 -> 32; matrix products, arithmetic and copies ran while one was open for 14% -> 35% of each run, Pallas kernels for 0% -> 0%
where the time goes in v1:
time: 631 us; the launch traced here: 624 us
  waiting for transfers between devices  193 us (31%)
  local copies, waits for them, and re-layouts  132 us (21%)
  starting transfers between devices  113 us (18%)
  matrix products  113 us (18%)
  other arithmetic  69.8 us (11%)
    ppermute x80, waiting for transfers between devices, swap(): return lax.ppermute(tensor, 'dp', [(i, i ^ bit) for i in range(count)])  126 us
    dot_general x18, matrix products, mm(): return lax.dot_general(a, b, (dims, ((), ())), preferred_element_type=F32)  107 us
    ppermute x80, starting transfers between devices, swap(): return lax.ppermute(tensor, 'dp', [(i, i ^ bit) for i in range(count)])  54.4 us
    ppermute x18, starting transfers between devices, from_ahead(): lax.ppermute(tensor, 'mp', [(i, (i - step) % count) for i in range(count)])  41.5 us
    ppermute x18, waiting for transfers between devices, from_ahead(): lax.ppermute(tensor, 'mp', [(i, (i - step) % count) for i in range(count)])  38.5 us
    ppermute x12, waiting for transfers between devices, from_behind(): lax.ppermute(tensor, 'mp', [(i, (i + step) % count) for i in range(count)])  27.5 us
    dynamic_update_slice x60, local copies, waits for them, and re-layouts, assemble(): whole = lax.dynamic_update_slice(whole, held[k], ((me ^ k) * share, column))  26.4 us
    unnamed x274, local copies, waits for them, and re-layouts  20.2 us
  transfers between devices with their start and end apart: 110, of which 32 were waited for; matrix products, arithmetic and copies ran while one was open for 35% of the time, Pallas kernels for 0%

profile of v1, /device:TPU:0, one launch (start us, length us, event | category | flops | bytes accessed | tf_op | source)
XLA Modules:
  0.0 623.9 jit_solution(12159059350902666646)
XLA Ops:
  1.7 3.1 collective-permute-start.20
  22.5 3.5 fusion.121
  29.9 3.2 constant_dynamic-slice_fusion.12
  37.0 3.0 collective-permute-start.12
  41.7 3.9 concatenate.117
  45.8 3.5 collective-permute-start.29
  55.6 11.2 %collective-permute-done.22 = bf16[144,512]{1,0:T(8,128)(2,1)S(1)} collective-permute-done((bf16[144,512]{1,0:T(8,128)(2,1)S(1)}, bf16[144,512]{1,0:T(8,128)(2,1)S(1)}, u32[]{:S(2)}, u32[]{:S(2)}) %collective-permute-start.22) | collective-permute-done | bytes 147488 | tf_op jit(solution)/shard_map/ppermute | solution.py:53
  68.9 5.4 collective-permute-done.4
  81.7 3.2 collective-permute-done.14
  96.9 5.1 collective-permute-done.8
  108.2 14.4 %collective-permute-done.57 = bf16[144,896]{1,0:T(8,128)(2,1)S(1)} collective-permute-done((bf16[144,896]{1,0:T(8,128)(2,1)S(1)}, bf16[144,896]{1,0:T(8,128)(2,1)S(1)}, u32[]{:S(2)}, u32[]{:S(2)}) %collective-permute-start.57) | collective-permute-done | bytes 258080 | tf_op jit(solution)/shard_map/ppermute | solution.py:53
  127.6 4.6 collective-permute-done.59
  141.9 3.5 collective-permute-done.35
  155.2 4.9 fusion.59
  189.8 5.0 collective-permute-done.52
  195.1 4.7 collective-permute-done.62
  203.4 5.0 collective-permute-done.66
  213.5 27.5 %collective-permute-done.38 = bf16[256,1152]{1,0:T(8,128)(2,1)S(1)} collective-permute-done((bf16[256,1152]{1,0:T(8,128)(2,1)S(1)}, bf16[256,1152]{1,0:T(8,128)(2,1)S(1)}, u32[]{:S(2)}, u32[]{:S(2)}) %collective-permute-start.38) | collective-permute-done | bytes 589856 | tf_op jit(solution)/shard_map/ppermute | solution.py:58
  241.0 11.2 %fusion.124 = f32[1024,1728]{0,1:T(8,128)} fusion(bf16[1152,1728]{1,0:T(8,128)(2,1)} %constant_dynamic-update-slice_fusion.16, bf16[256,1152]{1,0:T(8,128)(2,1)S(1)} %collective-permute-done.39, bf16[256,1152]{1,0:T(8,128)(2,1)S(1)} %collective-permute-done.38, bf16[256,1152]{1,0:T(8,128)(2,1)S(1)} %collective-permute-done.37, ...), kind=kOutput, calls=%fused_computation.386 | convolution fusion | flops 4086300672 | bytes 13418496 | tf_op jit(solution)/shard_map/dot_general | solution.py:16
  252.3 8.6 %fusion.123 = f32[1024,1728]{0,1:T(8,128)} fusion(bf16[1152,1728]{1,0:T(8,128)(2,1)S(1)} %constant_dynamic-update-slice_fusion.8, bf16[256,1152]{1,0:T(8,128)(2,1)S(1)} %collective-permute-done.39, bf16[256,1152]{1,0:T(8,128)(2,1)S(1)} %collective-permute-done.38, bf16[256,1152]{1,0:T(8,128)(2,1)S(1)} %collective-permute-done.37, ...), kind=kOutput, calls=%fused_computation.385 | convolution fusion | flops 4086300672 | bytes 13418496 | tf_op jit(solution)/shard_map/dot_general | solution.py:16
  260.9 19.1 %fusion.7 = (bf16[1024,1728]{0,1:T(8,128)(2,1)}, bf16[1024,1728]{0,1:T(8,128)(2,1)}, bf16[1024,1728]{0,1:T(8,128)(2,1)}) fusion(f32[1024,1728]{0,1:T(8,128)} %fusion.124, f32[1024,1728]{0,1:T(8,128)} %fusion.123, bf16[1152,1728]{1,0:T(8,128)(2,1)} %constant_dynamic-update-slice_fusion.50, bf16[256,1152]{1,0:T(8,128)(2,1)S(1)} %copy-done.65, ...), kind=kOutput, calls=%fused_computation.12 | convolution fusion | flops 4132306944 | bytes 31113216 | tf_op jit(solution)/shard_map/dot_general | solution.py:16
  280.0 10.6 %fusion.141 = (bf16[1024,1152]{1,0:T(8,128)(2,1)S(1)}, f32[1024,1152]{1,0:T(8,128)}) fusion(bf16[1024,1728]{0,1:T(8,128)(2,1)} %get-tuple-element.139, bf16[1152,1728]{1,0:T(8,128)(2,1)} %constant_dynamic-update-slice_fusion.50), kind=kOutput, calls=%fused_computation.400 | convolution fusion | flops 4078043136 | bytes 14598144 | tf_op jit(solution)/shard_map/dot_general | solution.py:16
  290.6 5.0 convolution_convert_fusion
  300.4 5.0 fusion.142
  305.5 9.5 %fusion.140 = (bf16[1024,1152]{1,0:T(8,128)(2,1)S(1)}, f32[1024,1152]{1,0:T(8,128)}) fusion(f32[1024,1152]{1,0:T(8,128)S(1)} %fusion.142, bf16[1024,1728]{0,1:T(8,128)(2,1)S(1)} %copy-done.132, bf16[1152,1728]{1,0:T(8,128)(2,1)} %constant_dynamic-update-slice_fusion.16), kind=kOutput, calls=%fused_computation.399 | convolution fusion | flops 4079222784 | bytes 19316736 | tf_op jit(solution)/shard_map/dot_general | solution.py:16
  323.4 6.3 %convolution_convert_fusion.1 = bf16[1152,1728]{0,1:T(8,128)(2,1)} fusion(bf16[1024,1728]{0,1:T(8,128)(2,1)S(1)} %copy-done.134, bf16[256,1152]{1,0:T(8,128)(2,1)S(1)} %copy-done.127, bf16[256,1152]{1,0:T(8,128)(2,1)S(1)} %copy-done.129, bf16[256,1152]{1,0:T(8,128)(2,1)S(1)} %copy-done.131, bf16[256,1152]{1,0:T(8,128)(2,1)S(1)} %multiply_convert_fusion.4), kind=kOutput, calls=%fused_computation.4 | convolution fusion | flops 4088291328 | bytes 9879552 | tf_op jit(solution)/shard_map/dot_general | solution.py:16
  329.7 6.5 %copy.221 = bf16[1152,1728]{1,0:T(8,128)(2,1)} copy(bf16[1152,1728]{0,1:T(8,128)(2,1)} %convolution_convert_fusion.1) | data formatting | bytes 7962624 | tf_op jit(solution)/shard_map/convert_element_type | solution.py:259
  336.1 9.5 %convolution_convert_fusion.2 = bf16[1152,1728]{0,1:T(8,128)(2,1)} fusion(bf16[1024,1728]{0,1:T(8,128)(2,1)} %get-tuple-element.137, bf16[256,1152]{1,0:T(8,128)(2,1)} %copy-done.126, bf16[256,1152]{1,0:T(8,128)(2,1)} %copy-done.128, bf16[256,1152]{1,0:T(8,128)(2,1)} %copy-done.130, bf16[256,1152]{1,0:T(8,128)(2,1)} %copy-done.61), kind=kOutput, calls=%fused_computation.5 | convolution fusion | flops 4088291328 | bytes 9879552 | tf_op jit(solution)/shard_map/dot_general | solution.py:16
  347.0 6.4 %copy.220 = bf16[1152,1728]{1,0:T(8,128)(2,1)} copy(bf16[1152,1728]{0,1:T(8,128)(2,1)} %convolution_convert_fusion.2) | data formatting | bytes 7962624 | tf_op jit(solution)/shard_map/convert_element_type | solution.py:258
  353.5 4.0 copy.224
  357.5 4.1 copy.223
  363.9 3.2 dynamic-slice_bitcast_fusion.1
  367.0 3.4 collective-permute-start.68
  372.0 3.0 multiply_reduce_fusion.4
  375.0 33.4 %collective-permute-done.69 = bf16[256,1152]{1,0:T(8,128)(2,1)} collective-permute-done((bf16[256,1152]{1,0:T(8,128)(2,1)}, bf16[256,1152]{1,0:T(8,128)(2,1)}, u32[]{:S(2)}, u32[]{:S(2)}) %collective-permute-start.69) | collective-permute-done | bytes 589856 | tf_op jit(solution)/shard_map/ppermute | solution.py:63
  408.4 4.0 multiply_add_fusion.2
  423.3 3.0 fusion.55
  431.2 5.8 fusion.129
  437.9 13.0 %collective-permute-start.76 = (bf16[256,512]{0,1:T(8,128)(2,1)}, bf16[256,512]{0,1:T(8,128)(2,1)}, u32[]{:S(2)}, u32[]{:S(2)}) collective-permute-start(bf16[256,512]{0,1:T(8,128)(2,1)} %get-tuple-element.183), channel_id=1, source_target_pairs={{0,1},{1,2},{2,3},{3,0},{4,5},{5,6},{6,7},{7,4},{8,9},{9,10},{10,1... | collective-permute-start | bytes 786440 | tf_op jit(solution)/shard_map/ppermute | solution.py:63
  467.5 4.0 copy.228
  510.5 3.2 collective-permute-done.88
  520.5 5.5 collective-permute-done.89
  527.4 3.8 collective-permute-done.85
  560.6 3.4 collective-permute-done.108
  576.1 22.5 %collective-permute-done.79 = bf16[144,1024]{1,0:T(8,128)(2,1)S(1)} collective-permute-done((bf16[144,1024]{1,0:T(8,128)(2,1)S(1)}, bf16[144,1024]{1,0:T(8,128)(2,1)S(1)}, u32[]{:S(2)}, u32[]{:S(2)}) %collective-permute-start.79) | collective-permute-done | bytes 294944 | tf_op jit(solution)/shard_map/ppermute | solution.py:53
  598.7 4.7 collective-permute-start.82
  610.9 6.6 %collective-permute-done.97 = bf16[144,1728]{1,0:T(8,128)(2,1)S(1)} collective-permute-done((bf16[144,1728]{1,0:T(8,128)(2,1)S(1)}, bf16[144,1728]{1,0:T(8,128)(2,1)S(1)}, u32[]{:S(2)}, u32[]{:S(2)}) %collective-permute-start.97) | collective-permute-done | bytes 497696 | tf_op jit(solution)/shard_map/ppermute | solution.py:53
  619.2 4.4 add_multiply_fusion
  (685 shorter events, 272.8 us)
Async XLA Ops:
  1.7 50.4 %collective-permute-start.20 = (bf16[144,256]{1,0:T(8,128)(2,1)S(1)}, bf16[144,256]{1,0:T(8,128)(2,1)}, u32[]{:S(2)}, u32[]{:S(2)}) collective-permute-start(bf16[144,256]{1,0:T(8,128)(2,1)S(1)} %convert_bitcast_fusion.2), channel_id=1, source_target_pairs={{0,1},{1,2},{2,3},{3,0},{4,5},{5,6},{6,7},{7,4},{8,9},{9,10},{10,1... | collective-permute-start | bytes 221192 | tf_op jit(solution)/shard_map/ppermute | solution.py:58
  4.8 48.8 %collective-permute-start.28 = (bf16[144,256]{1,0:T(8,128)(2,1)S(1)}, bf16[144,256]{1,0:T(8,128)(2,1)}, u32[]{:S(2)}, u32[]{:S(2)}) collective-permute-start(bf16[144,256]{1,0:T(8,128)(2,1)S(1)} %convert_bitcast_fusion.2), channel_id=1, source_target_pairs={{0,2},{1,3},{2,0},{3,1},{4,6},{5,7},{6,4},{7,5},{8,10},{9,11},{10,... | collective-permute-start | bytes 221192 | tf_op jit(solution)/shard_map/ppermute | solution.py:58
  9.5 27.6 %collective-permute-start = (bf16[36,640]{1,0:T(8,128)(2,1)S(1)}, bf16[36,640]{1,0:T(8,128)(2,1)S(1)}, u32[]{:S(2)}, u32[]{:S(2)}) collective-permute-start(bf16[36,640]{1,0:T(8,128)(2,1)S(1)} %concatenate.116), channel_id=1, source_target_pairs={{0,3},{1,0},{2,1},{3,2},{4,7},{5,4},{6,5},{7,6},{8,11},{9,8},{10,9... | collective-permute-start | bytes 138248 | tf_op jit(solution)/shard_map/ppermute | solution.py:58
  10.9 29.2 %collective-permute-start.1 = (bf16[36,640]{1,0:T(8,128)(2,1)S(1)}, bf16[36,640]{1,0:T(8,128)(2,1)}, u32[]{:S(2)}, u32[]{:S(2)}) collective-permute-start(bf16[36,640]{1,0:T(8,128)(2,1)S(1)} %concatenate.116), channel_id=1, source_target_pairs={{0,2},{1,3},{2,0},{3,1},{4,6},{5,7},{6,4},{7,5},{8,10},{9,11},{10,... | collective-permute-start | bytes 138248 | tf_op jit(solution)/shard_map/ppermute | solution.py:58
  11.1 29.9 %collective-permute-start.2 = (bf16[36,640]{1,0:T(8,128)(2,1)S(1)}, bf16[36,640]{1,0:T(8,128)(2,1)}, u32[]{:S(2)}, u32[]{:S(2)}) collective-permute-start(bf16[36,640]{1,0:T(8,128)(2,1)S(1)} %concatenate.116), channel_id=1, source_target_pairs={{0,1},{1,2},{2,3},{3,0},{4,5},{5,6},{6,7},{7,4},{8,9},{9,10},{10,1... | collective-permute-start | bytes 138248 | tf_op jit(solution)/shard_map/ppermute | solution.py:58
  49.2 54.3 %collective-permute-start.40 = (bf16[144,1728]{1,0:T(8,128)(2,1)}, bf16[144,1728]{1,0:T(8,128)(2,1)S(1)}, u32[]{:S(2)}, u32[]{:S(2)}) collective-permute-start(bf16[144,1728]{1,0:T(8,128)(2,1)} %get-tuple-element.185), channel_id=1, source_target_pairs={{0,4},{4,0},{8,12},{12,8},{16,20},{20,16},{24,28},{28,24},{1,5},{5... | collective-permute-start | bytes 1493000 | tf_op jit(solution)/shard_map/ppermute | solution.py:53
  49.3 56.6 %collective-permute-start.41 = (bf16[144,1728]{1,0:T(8,128)(2,1)}, bf16[144,1728]{1,0:T(8,128)(2,1)S(1)}, u32[]{:S(2)}, u32[]{:S(2)}) collective-permute-start(bf16[144,1728]{1,0:T(8,128)(2,1)} %get-tuple-element.185), channel_id=1, source_target_pairs={{0,8},{4,12},{8,0},{12,4},{16,24},{20,28},{24,16},{28,20},{1,9},{5... | collective-permute-start | bytes 1493000 | tf_op jit(solution)/shard_map/ppermute | solution.py:53
  52.2 22.2 %collective-permute-start.54 = (bf16[144,896]{1,0:T(8,128)(2,1)S(1)}, bf16[144,896]{1,0:T(8,128)(2,1)S(1)}, u32[]{:S(2)}, u32[]{:S(2)}) collective-permute-start(bf16[144,896]{1,0:T(8,128)(2,1)S(1)} %get-tuple-element.200), channel_id=1, source_target_pairs={{0,4},{4,0},{8,12},{12,8},{16,20},{20,16},{24,28},{28,24},{1,5},{5... | collective-permute-start | bytes 774152 | tf_op jit(solution)/shard_map/ppermute | solution.py:53
  92.3 87.6 %collective-permute-start.43 = (bf16[144,1728]{1,0:T(8,128)(2,1)}, bf16[144,1728]{1,0:T(8,128)(2,1)}, u32[]{:S(2)}, u32[]{:S(2)}) collective-permute-start(bf16[144,1728]{1,0:T(8,128)(2,1)} %get-tuple-element.185), channel_id=1, source_target_pairs={{0,16},{4,20},{8,24},{12,28},{16,0},{20,4},{24,8},{28,12},{1,17},{... | collective-permute-start | bytes 1493000 | tf_op jit(solution)/shard_map/ppermute | solution.py:53
  102.0 20.6 %collective-permute-start.48 = (bf16[144,1728]{1,0:T(8,128)(2,1)}, bf16[144,1728]{1,0:T(8,128)(2,1)S(1)}, u32[]{:S(2)}, u32[]{:S(2)}) collective-permute-start(bf16[144,1728]{1,0:T(8,128)(2,1)} %get-tuple-element.186), channel_id=1, source_target_pairs={{0,8},{4,12},{8,0},{12,4},{16,24},{20,28},{24,16},{28,20},{1,9},{5... | collective-permute-start | bytes 1493000 | tf_op jit(solution)/shard_map/ppermute | solution.py:53
  103.6 64.2 %collective-permute-start.50 = (bf16[144,1728]{1,0:T(8,128)(2,1)}, bf16[144,1728]{1,0:T(8,128)(2,1)}, u32[]{:S(2)}, u32[]{:S(2)}) collective-permute-start(bf16[144,1728]{1,0:T(8,128)(2,1)} %get-tuple-element.186), channel_id=1, source_target_pairs={{0,16},{4,20},{8,24},{12,28},{16,0},{20,4},{24,8},{28,12},{1,17},{... | collective-permute-start | bytes 1493000 | tf_op jit(solution)/shard_map/ppermute | solution.py:53
  105.9 16.7 %collective-permute-start.57 = (bf16[144,896]{1,0:T(8,128)(2,1)S(1)}, bf16[144,896]{1,0:T(8,128)(2,1)S(1)}, u32[]{:S(2)}, u32[]{:S(2)}) collective-permute-start(bf16[144,896]{1,0:T(8,128)(2,1)S(1)} %get-tuple-element.200), channel_id=1, source_target_pairs={{0,16},{4,20},{8,24},{12,28},{16,0},{20,4},{24,8},{28,12},{1,17},{... | collective-permute-start | bytes 774152 | tf_op jit(solution)/shard_map/ppermute | solution.py:53
  107.4 16.6 %collective-permute-start.56 = (bf16[144,896]{1,0:T(8,128)(2,1)S(1)}, bf16[144,896]{1,0:T(8,128)(2,1)S(1)}, u32[]{:S(2)}, u32[]{:S(2)}) collective-permute-start(bf16[144,896]{1,0:T(8,128)(2,1)S(1)} %collective-permute-done.55), channel_id=1, source_target_pairs={{0,4},{4,0},{8,12},{12,8},{16,20},{20,16},{24,28},{28,24},{1,5},{5... | collective-permute-start | bytes 774152 | tf_op jit(solution)/shard_map/ppermute | solution.py:53
  146.8 14.2 %collective-permute-start.15 = (bf16[144,1024]{1,0:T(8,128)(2,1)}, bf16[144,1024]{1,0:T(8,128)(2,1)}, u32[]{:S(2)}, u32[]{:S(2)}) collective-permute-start(bf16[144,1024]{1,0:T(8,128)(2,1)} %collective-permute-done.14), channel_id=1, source_target_pairs={{0,4},{4,0},{8,12},{12,8},{16,20},{20,16},{24,28},{28,24},{1,5},{5... | collective-permute-start | bytes 884744 | tf_op jit(solution)/shard_map/ppermute | solution.py:53
  146.9 17.7 %collective-permute-start.18 = (bf16[144,1024]{1,0:T(8,128)(2,1)}, bf16[144,1024]{1,0:T(8,128)(2,1)}, u32[]{:S(2)}, u32[]{:S(2)}) collective-permute-start(bf16[144,1024]{1,0:T(8,128)(2,1)} %collective-permute-done.14), channel_id=1, source_target_pairs={{0,16},{4,20},{8,24},{12,28},{16,0},{20,4},{24,8},{28,12},{1,17},{... | collective-permute-start | bytes 884744 | tf_op jit(solution)/shard_map/ppermute | solution.py:53
  148.5 14.9 %collective-permute-start.17 = (bf16[144,1024]{1,0:T(8,128)(2,1)}, bf16[144,1024]{1,0:T(8,128)(2,1)}, u32[]{:S(2)}, u32[]{:S(2)}) collective-permute-start(bf16[144,1024]{1,0:T(8,128)(2,1)} %collective-permute-done.16), channel_id=1, source_target_pairs={{0,4},{4,0},{8,12},{12,8},{16,20},{20,16},{24,28},{28,24},{1,5},{5... | collective-permute-start | bytes 884744 | tf_op jit(solution)/shard_map/ppermute | solution.py:53
  163.4 18.0 %collective-permute-start.42 = (bf16[144,1728]{1,0:T(8,128)(2,1)}, bf16[144,1728]{1,0:T(8,128)(2,1)S(1)}, u32[]{:S(2)}, u32[]{:S(2)}) collective-permute-start(bf16[144,1728]{1,0:T(8,128)(2,1)} %copy-done.79), channel_id=1, source_target_pairs={{0,4},{4,0},{8,12},{12,8},{16,20},{20,16},{24,28},{28,24},{1,5},{5... | collective-permute-start | bytes 1493000 | tf_op jit(solution)/shard_map/ppermute | solution.py:53
  164.6 22.6 %collective-permute-start.45 = (bf16[144,1728]{1,0:T(8,128)(2,1)}, bf16[144,1728]{1,0:T(8,128)(2,1)S(1)}, u32[]{:S(2)}, u32[]{:S(2)}) collective-permute-start(bf16[144,1728]{1,0:T(8,128)(2,1)} %copy-done.79), channel_id=1, source_target_pairs={{0,16},{4,20},{8,24},{12,28},{16,0},{20,4},{24,8},{28,12},{1,17},{... | collective-permute-start | bytes 1493000 | tf_op jit(solution)/shard_map/ppermute | solution.py:53
  167.8 16.5 %collective-permute-start.49 = (bf16[144,1728]{1,0:T(8,128)(2,1)S(1)}, bf16[144,1728]{1,0:T(8,128)(2,1)S(1)}, u32[]{:S(2)}, u32[]{:S(2)}) collective-permute-start(bf16[144,1728]{1,0:T(8,128)(2,1)S(1)} %copy-done.81), channel_id=1, source_target_pairs={{0,4},{4,0},{8,12},{12,8},{16,20},{20,16},{24,28},{28,24},{1,5},{5... | collective-permute-start | bytes 1493000 | tf_op jit(solution)/shard_map/ppermute | solution.py:53
  168.3 21.3 %collective-permute-start.51 = (bf16[144,1728]{1,0:T(8,128)(2,1)}, bf16[144,1728]{1,0:T(8,128)(2,1)S(1)}, u32[]{:S(2)}, u32[]{:S(2)}) collective-permute-start(bf16[144,1728]{1,0:T(8,128)(2,1)} %collective-permute-done.50), channel_id=1, source_target_pairs={{0,4},{4,0},{8,12},{12,8},{16,20},{20,16},{24,28},{28,24},{1,5},{5... | collective-permute-start | bytes 1493000 | tf_op jit(solution)/shard_map/ppermute | solution.py:53
  179.9 14.8 %collective-permute-start.52 = (bf16[144,1728]{1,0:T(8,128)(2,1)}, bf16[144,1728]{1,0:T(8,128)(2,1)S(1)}, u32[]{:S(2)}, u32[]{:S(2)}) collective-permute-start(bf16[144,1728]{1,0:T(8,128)(2,1)} %collective-permute-done.50), channel_id=1, source_target_pairs={{0,8},{4,12},{8,0},{12,4},{16,24},{20,28},{24,16},{28,20},{1,9},{5... | collective-permute-start | bytes 1493000 | tf_op jit(solution)/shard_map/ppermute | solution.py:53
  184.3 17.0 %collective-permute-start.61 = (bf16[144,832]{1,0:T(8,128)(2,1)S(1)}, bf16[144,832]{1,0:T(8,128)(2,1)S(1)}, u32[]{:S(2)}, u32[]{:S(2)}) collective-permute-start(bf16[144,832]{1,0:T(8,128)(2,1)S(1)} %get-tuple-element.198), channel_id=1, source_target_pairs={{0,4},{4,0},{8,12},{12,8},{16,20},{20,16},{24,28},{28,24},{1,5},{5... | collective-permute-start | bytes 718856 | tf_op jit(solution)/shard_map/ppermute | solution.py:53
  185.8 13.9 %collective-permute-start.62 = (bf16[144,832]{1,0:T(8,128)(2,1)S(1)}, bf16[144,832]{1,0:T(8,128)(2,1)S(1)}, u32[]{:S(2)}, u32[]{:S(2)}) collective-permute-start(bf16[144,832]{1,0:T(8,128)(2,1)S(1)} %get-tuple-element.198), channel_id=1, source_target_pairs={{0,8},{4,12},{8,0},{12,4},{16,24},{20,28},{24,16},{28,20},{1,9},{5... | collective-permute-start | bytes 718856 | tf_op jit(solution)/shard_map/ppermute | solution.py:53
  189.6 23.9 %collective-permute-start.39 = (bf16[256,1152]{1,0:T(8,128)(2,1)S(1)}, bf16[256,1152]{1,0:T(8,128)(2,1)S(1)}, u32[]{:S(2)}, u32[]{:S(2)}) collective-permute-start(bf16[256,1152]{1,0:T(8,128)(2,1)S(1)} %multiply_convert_fusion.4), channel_id=1, source_target_pairs={{0,3},{1,0},{2,1},{3,2},{4,7},{5,4},{6,5},{7,6},{8,11},{9,8},{10,9... | collective-permute-start | bytes 1769480 | tf_op jit(solution)/shard_map/ppermute | solution.py:58
  194.7 46.3 %collective-permute-start.38 = (bf16[256,1152]{1,0:T(8,128)(2,1)S(1)}, bf16[256,1152]{1,0:T(8,128)(2,1)S(1)}, u32[]{:S(2)}, u32[]{:S(2)}) collective-permute-start(bf16[256,1152]{1,0:T(8,128)(2,1)S(1)} %multiply_convert_fusion.4), channel_id=1, source_target_pairs={{0,2},{1,3},{2,0},{3,1},{4,6},{5,7},{6,4},{7,5},{8,10},{9,11},{10,... | collective-permute-start | bytes 1769480 | tf_op jit(solution)/shard_map/ppermute | solution.py:58
  211.9 29.1 %collective-permute-start.37 = (bf16[256,1152]{1,0:T(8,128)(2,1)S(1)}, bf16[256,1152]{1,0:T(8,128)(2,1)S(1)}, u32[]{:S(2)}, u32[]{:S(2)}) collective-permute-start(bf16[256,1152]{1,0:T(8,128)(2,1)S(1)} %multiply_convert_fusion.4), channel_id=1, source_target_pairs={{0,1},{1,2},{2,3},{3,0},{4,5},{5,6},{6,7},{7,4},{8,9},{9,10},{10,1... | collective-permute-start | bytes 1769480 | tf_op jit(solution)/shard_map/ppermute | solution.py:58
  316.2 50.9 %collective-permute-start.73 = (bf16[256,1152]{1,0:T(8,128)(2,1)}, bf16[256,1152]{1,0:T(8,128)(2,1)}, u32[]{:S(2)}, u32[]{:S(2)}) collective-permute-start(bf16[256,1152]{1,0:T(8,128)(2,1)} %get-tuple-element.151), channel_id=1, source_target_pairs={{0,1},{1,2},{2,3},{3,0},{4,5},{5,6},{6,7},{7,4},{8,9},{9,10},{10,1... | collective-permute-start | bytes 1769480 | tf_op jit(solution)/shard_map/ppermute | solution.py:63
  316.7 54.8 %collective-permute-start.72 = (bf16[256,1152]{1,0:T(8,128)(2,1)}, bf16[256,1152]{1,0:T(8,128)(2,1)}, u32[]{:S(2)}, u32[]{:S(2)}) collective-permute-start(bf16[256,1152]{1,0:T(8,128)(2,1)} %get-tuple-element.152), channel_id=1, source_target_pairs={{0,2},{1,3},{2,0},{3,1},{4,6},{5,7},{6,4},{7,5},{8,10},{9,11},{10,... | collective-permute-start | bytes 1769480 | tf_op jit(solution)/shard_map/ppermute | solution.py:63
  318.7 52.8 %collective-permute-start.71 = (bf16[256,1152]{1,0:T(8,128)(2,1)}, bf16[256,1152]{1,0:T(8,128)(2,1)}, u32[]{:S(2)}, u32[]{:S(2)}) collective-permute-start(bf16[256,1152]{1,0:T(8,128)(2,1)} %get-tuple-element.150), channel_id=1, source_target_pairs={{0,3},{1,0},{2,1},{3,2},{4,7},{5,4},{6,5},{7,6},{8,11},{9,8},{10,9... | collective-permute-start | bytes 1769480 | tf_op jit(solution)/shard_map/ppermute | solution.py:63
  322.8 52.2 %collective-permute-start.70 = (bf16[256,1152]{1,0:T(8,128)(2,1)}, bf16[256,1152]{1,0:T(8,128)(2,1)}, u32[]{:S(2)}, u32[]{:S(2)}) collective-permute-start(bf16[256,1152]{1,0:T(8,128)(2,1)} %get-tuple-element.158), channel_id=1, source_target_pairs={{0,1},{1,2},{2,3},{3,0},{4,5},{5,6},{6,7},{7,4},{8,9},{9,10},{10,1... | collective-permute-start | bytes 1769480 | tf_op jit(solution)/shard_map/ppermute | solution.py:63
  322.8 85.6 %collective-permute-start.69 = (bf16[256,1152]{1,0:T(8,128)(2,1)}, bf16[256,1152]{1,0:T(8,128)(2,1)}, u32[]{:S(2)}, u32[]{:S(2)}) collective-permute-start(bf16[256,1152]{1,0:T(8,128)(2,1)} %get-tuple-element.159), channel_id=1, source_target_pairs={{0,2},{1,3},{2,0},{3,1},{4,6},{5,7},{6,4},{7,5},{8,10},{9,11},{10,... | collective-permute-start | bytes 1769480 | tf_op jit(solution)/shard_map/ppermute | solution.py:63
  367.0 41.4 %collective-permute-start.68 = (bf16[256,1152]{1,0:T(8,128)(2,1)S(1)}, bf16[256,1152]{1,0:T(8,128)(2,1)S(1)}, u32[]{:S(2)}, u32[]{:S(2)}) collective-permute-start(bf16[256,1152]{1,0:T(8,128)(2,1)S(1)} %copy-done.62), channel_id=1, source_target_pairs={{0,3},{1,0},{2,1},{3,2},{4,7},{5,4},{6,5},{7,6},{8,11},{9,8},{10,9... | collective-permute-start | bytes 1769480 | tf_op jit(solution)/shard_map/ppermute | solution.py:63
  371.5 195.6 %collective-permute-start.95 = (bf16[2,2,144,1728]{3,2,1,0:T(8,128)(2,1)}, bf16[2,2,144,1728]{3,2,1,0:T(8,128)(2,1)}, u32[]{:S(2)}, u32[]{:S(2)}) collective-permute-start(bf16[2,2,144,1728]{3,2,1,0:T(8,128)(2,1)} %dynamic-slice_bitcast_fusion), channel_id=1, source_target_pairs={{0,4},{4,0},{8,12},{12,8},{16,20},{20,16},{24,28},{28,24},{1,5},{5... | collective-permute-start | bytes 5971976 | tf_op jit(solution)/shard_map/ppermute | solution.py:53
  371.5 117.0 %collective-permute-start.101 = (bf16[2,2,144,832]{3,2,1,0:T(8,128)(2,1)}, bf16[2,2,144,832]{3,2,1,0:T(8,128)(2,1)}, u32[]{:S(2)}, u32[]{:S(2)}) collective-permute-start(bf16[2,2,144,832]{3,2,1,0:T(8,128)(2,1)} %dynamic-slice_bitcast_fusion.2), channel_id=1, source_target_pairs={{0,4},{4,0},{8,12},{12,8},{16,20},{20,16},{24,28},{28,24},{1,5},{5... | collective-permute-start | bytes 2875400 | tf_op jit(solution)/shard_map/ppermute | solution.py:53
  437.9 42.6 %collective-permute-start.76 = (bf16[256,512]{0,1:T(8,128)(2,1)}, bf16[256,512]{0,1:T(8,128)(2,1)}, u32[]{:S(2)}, u32[]{:S(2)}) collective-permute-start(bf16[256,512]{0,1:T(8,128)(2,1)} %get-tuple-element.183), channel_id=1, source_target_pairs={{0,1},{1,2},{2,3},{3,0},{4,5},{5,6},{6,7},{7,4},{8,9},{9,10},{10,1... | collective-permute-start | bytes 786440 | tf_op jit(solution)/shard_map/ppermute | solution.py:63
  450.9 29.7 %collective-permute-start.75 = (bf16[256,512]{0,1:T(8,128)(2,1)}, bf16[256,512]{0,1:T(8,128)(2,1)}, u32[]{:S(2)}, u32[]{:S(2)}) collective-permute-start(bf16[256,512]{0,1:T(8,128)(2,1)} %get-tuple-element.184), channel_id=1, source_target_pairs={{0,2},{1,3},{2,0},{3,1},{4,6},{5,7},{6,4},{7,5},{8,10},{9,11},{10,... | collective-permute-start | bytes 786440 | tf_op jit(solution)/shard_map/ppermute | solution.py:63
  453.6 27.5 %collective-permute-start.74 = (bf16[256,512]{0,1:T(8,128)(2,1)}, bf16[256,512]{0,1:T(8,128)(2,1)}, u32[]{:S(2)}, u32[]{:S(2)}) collective-permute-start(bf16[256,512]{0,1:T(8,128)(2,1)} %get-tuple-element.182), channel_id=1, source_target_pairs={{0,3},{1,0},{2,1},{3,2},{4,7},{5,4},{6,5},{7,6},{8,11},{9,8},{10,9... | collective-permute-start | bytes 786440 | tf_op jit(solution)/shard_map/ppermute | solution.py:63
  480.6 63.8 %collective-permute-start.77 = (bf16[2,2,144,1024]{3,2,0,1:T(8,128)(2,1)}, bf16[2,2,144,1024]{3,2,0,1:T(8,128)(2,1)}, u32[]{:S(2)}, u32[]{:S(2)}) collective-permute-start(bf16[2,2,144,1024]{3,2,0,1:T(8,128)(2,1)} %bitcast.283), channel_id=1, source_target_pairs={{0,4},{4,0},{8,12},{12,8},{16,20},{20,16},{24,28},{28,24},{1,5},{5... | collective-permute-start | bytes 3538952 | tf_op jit(solution)/shard_map/ppermute | solution.py:53
  493.1 14.9 %collective-permute-start.102 = (bf16[2,144,832]{2,1,0:T(8,128)(2,1)}, bf16[2,144,832]{2,1,0:T(8,128)(2,1)}, u32[]{:S(2)}, u32[]{:S(2)}) collective-permute-start(bf16[2,144,832]{2,1,0:T(8,128)(2,1)} %dynamic-slice_bitcast_fusion.8), channel_id=1, source_target_pairs={{0,16},{4,20},{8,24},{12,28},{16,0},{20,4},{24,8},{28,12},{1,17},{... | collective-permute-start | bytes 1437704 | tf_op jit(solution)/shard_map/ppermute | solution.py:53
  494.4 23.4 %collective-permute-start.99 = (bf16[2,144,896]{2,1,0:T(8,128)(2,1)}, bf16[2,144,896]{2,1,0:T(8,128)(2,1)}, u32[]{:S(2)}, u32[]{:S(2)}) collective-permute-start(bf16[2,144,896]{2,1,0:T(8,128)(2,1)} %dynamic-slice_bitcast_fusion.9), channel_id=1, source_target_pairs={{0,8},{4,12},{8,0},{12,4},{16,24},{20,28},{24,16},{28,20},{1,9},{5... | collective-permute-start | bytes 1548296 | tf_op jit(solution)/shard_map/ppermute | solution.py:53
  497.7 16.0 %collective-permute-start.88 = (bf16[2,144,512]{2,1,0:T(8,128)(2,1)}, bf16[2,144,512]{2,1,0:T(8,128)(2,1)S(1)}, u32[]{:S(2)}, u32[]{:S(2)}) collective-permute-start(bf16[2,144,512]{2,1,0:T(8,128)(2,1)} %dynamic-slice_bitcast_fusion.13), channel_id=1, source_target_pairs={{0,16},{4,20},{8,24},{12,28},{16,0},{20,4},{24,8},{28,12},{1,17},{... | collective-permute-start | bytes 884744 | tf_op jit(solution)/shard_map/ppermute | solution.py:53
  513.7 21.2 %collective-permute-start.105 = (bf16[2,144,640]{2,1,0:T(8,128)(2,1)}, bf16[2,144,640]{2,1,0:T(8,128)(2,1)S(1)}, u32[]{:S(2)}, u32[]{:S(2)}) collective-permute-start(bf16[2,144,640]{2,1,0:T(8,128)(2,1)} %bitcast.286), channel_id=1, source_target_pairs={{0,16},{4,20},{8,24},{12,28},{16,0},{20,4},{24,8},{28,12},{1,17},{... | collective-permute-start | bytes 1105928 | tf_op jit(solution)/shard_map/ppermute | solution.py:53
  516.3 17.5 %collective-permute-start.103 = (bf16[144,832]{1,0:T(8,128)(2,1)S(1)}, bf16[144,832]{1,0:T(8,128)(2,1)S(1)}, u32[]{:S(2)}, u32[]{:S(2)}) collective-permute-start(bf16[144,832]{1,0:T(8,128)(2,1)S(1)} %dynamic-slice_bitcast_fusion.16), channel_id=1, source_target_pairs={{0,8},{4,12},{8,0},{12,4},{16,24},{20,28},{24,16},{28,20},{1,9},{5... | collective-permute-start | bytes 718856 | tf_op jit(solution)/shard_map/ppermute | solution.py:53
  539.3 33.2 %collective-permute-start.92 = (bf16[2,2,144,1728]{3,2,1,0:T(8,128)(2,1)}, bf16[2,2,144,1728]{3,2,1,0:T(8,128)(2,1)}, u32[]{:S(2)}, u32[]{:S(2)}) collective-permute-start(bf16[2,2,144,1728]{3,2,1,0:T(8,128)(2,1)} %dynamic-slice_bitcast_fusion.1), channel_id=1, source_target_pairs={{0,4},{4,0},{8,12},{12,8},{16,20},{20,16},{24,28},{28,24},{1,5},{5... | collective-permute-start | bytes 5971976 | tf_op jit(solution)/shard_map/ppermute | solution.py:53
  550.3 13.8 %collective-permute-start.108 = (bf16[36,640]{0,1:T(8,128)(2,1)S(1)}, bf16[36,640]{0,1:T(8,128)(2,1)S(1)}, u32[]{:S(2)}, u32[]{:S(2)}) collective-permute-start(bf16[36,640]{0,1:T(8,128)(2,1)S(1)} %get-tuple-element.189), channel_id=1, source_target_pairs={{0,2},{1,3},{2,0},{3,1},{4,6},{5,7},{6,4},{7,5},{8,10},{9,11},{10,... | collective-permute-start | bytes 138248 | tf_op jit(solution)/shard_map/ppermute | solution.py:63
  569.9 35.9 %collective-permute-start.96 = (bf16[2,144,1728]{2,1,0:T(8,128)(2,1)S(1)}, bf16[2,144,1728]{2,1,0:T(8,128)(2,1)S(1)}, u32[]{:S(2)}, u32[]{:S(2)}) collective-permute-start(bf16[2,144,1728]{2,1,0:T(8,128)(2,1)S(1)} %dynamic-slice_bitcast_fusion.4), channel_id=1, source_target_pairs={{0,16},{4,20},{8,24},{12,28},{16,0},{20,4},{24,8},{28,12},{1,17},{... | collective-permute-start | bytes 2985992 | tf_op jit(solution)/shard_map/ppermute | solution.py:53
  571.6 26.9 %collective-permute-start.79 = (bf16[144,1024]{1,0:T(8,128)(2,1)S(1)}, bf16[144,1024]{1,0:T(8,128)(2,1)S(1)}, u32[]{:S(2)}, u32[]{:S(2)}) collective-permute-start(bf16[144,1024]{1,0:T(8,128)(2,1)S(1)} %dynamic-slice_bitcast_fusion.15), channel_id=1, source_target_pairs={{0,16},{4,20},{8,24},{12,28},{16,0},{20,4},{24,8},{28,12},{1,17},{... | collective-permute-start | bytes 884744 | tf_op jit(solution)/shard_map/ppermute | solution.py:53
  574.6 33.0 %collective-permute-start.93 = (bf16[2,144,1728]{2,1,0:T(8,128)(2,1)S(1)}, bf16[2,144,1728]{2,1,0:T(8,128)(2,1)S(1)}, u32[]{:S(2)}, u32[]{:S(2)}) collective-permute-start(bf16[2,144,1728]{2,1,0:T(8,128)(2,1)S(1)} %dynamic-slice_bitcast_fusion.5), channel_id=1, source_target_pairs={{0,8},{4,12},{8,0},{12,4},{16,24},{20,28},{24,16},{28,20},{1,9},{5... | collective-permute-start | bytes 2985992 | tf_op jit(solution)/shard_map/ppermute | solution.py:53
  (197 other events, 1721.6 us)

commit v2 on v1

v2 whole, which is shorter than its diff:
```python
import jax
import jax.numpy as jnp
from jax import lax
from jax.experimental import pallas as pl
from jax.experimental.pallas import tpu as pltpu
from jax.sharding import PartitionSpec as P

HD = 256
LANES = 128
TILE = 256
VMEM_BYTES = 56 * 1024 * 1024
EPSILON = 1e-06
MOMENTUM = 0.9
AVERAGING = 0.5
BF = jnp.bfloat16
F32 = jnp.float32


def mm(a, b, dims):
    return lax.dot_general(a, b, (dims, ((), ())), preferred_element_type=F32)


def inverse_rms(tensor):
    return lax.rsqrt(jnp.mean(tensor * tensor, axis=-1, keepdims=True) + EPSILON)


def norm_back(grad_in, unit, inverse, gain_vec):
    scaled = grad_in * gain_vec
    return inverse * (scaled - unit * jnp.mean(scaled * unit, axis=-1, keepdims=True))


def rotation(length, head_size):
    halfway = head_size // 2
    frequency = 1000000.0 ** (-(jnp.arange(halfway).astype(F32) * 2.0 / head_size))
    angles = jnp.arange(length).astype(F32)[:, None] * frequency[None, :]
    return (jnp.cos(angles), jnp.sin(angles))


def rotate(tensor, cosine, sine_tab):
    halfway = tensor.shape[-1] // 2
    former = tensor[..., :halfway]
    latter = tensor[..., halfway:]
    return jnp.concatenate(
        [former * cosine - latter * sine_tab, latter * cosine + former * sine_tab], axis=-1
    )


def advance(gradient, moment, average, weight, step_rate):
    moment_new = MOMENTUM * moment + gradient
    weight_new = weight - step_rate * (gradient + MOMENTUM * moment_new)
    average_new = AVERAGING * average + (1.0 - AVERAGING) * weight_new
    return (gradient, moment_new, average_new, weight_new)


def swap(tensor, bit):
    count = lax.axis_size("dp")
    return lax.ppermute(tensor, "dp", [(i, i ^ bit) for i in range(count)])


def across_heads(tensor, bit):
    count = lax.axis_size("mp")
    return lax.ppermute(tensor, "mp", [(i, i ^ bit) for i in range(count)])


def bit_orders():
    bits = []
    while 2 ** len(bits) < lax.axis_size("dp"):
        bits.append(2 ** len(bits))
    outer = bits[1:]
    return (outer + bits[:1], outer[::-1] + bits[:1])


def split_three(tensor):
    high = lax.reduce_precision(tensor, 8, 7)
    rest = tensor - high
    middle = lax.reduce_precision(rest, 8, 7)
    return [high.astype(BF), middle.astype(BF), (rest - middle).astype(BF)]


def spread_on(pieces, order):
    held, offsets = jnp.concatenate(pieces, axis=0), [0, order[0]]
    for bit in order[1:-1]:
        held = jnp.concatenate([held, swap(held, bit)], axis=0)
        offsets = offsets + [k ^ bit for k in offsets]
    return [held, offsets]


def spread_out(group, order):
    held, offsets = group
    bit = order[-1]
    return [(held, offsets), (swap(held, bit), [k ^ bit for k in offsets])]


def spread_direct(tensor):
    offsets = list(range(0, lax.axis_size("dp"), 2))
    pieces = [tensor] + [swap(tensor, k) for k in offsets[1:]]
    held = jnp.concatenate(pieces, axis=0)
    return [(held, offsets), (swap(held, 1), [k + 1 for k in offsets])]


def spread_wide(pieces, second, order):
    offsets = [0, order[0]]
    for bit in order[1:-1]:
        sent = [swap(piece, bit) for piece in (second if len(pieces) == 2 else pieces)]
        pieces = pieces + sent
        offsets = offsets + [k ^ bit for k in offsets]
    return pieces, offsets


def spread_last(pieces, offsets, bit):
    pair = jnp.concatenate(pieces, axis=0)
    return [(pair, offsets), (swap(pair, bit), [k ^ bit for k in offsets])]


def round_up(number, unit):
    return -(-number // unit) * unit


def column_cuts(width):
    half = round_up(width // TILE, 2) // 2 * TILE
    first = round_up(half // TILE, 2) // 2 * TILE
    return half, [(0, first), (first, half), (half, width)]


def lay(groups):
    share = groups[0][0].shape[0] // len(groups[0][1])
    if share % 16 == 0:
        return groups
    me = lax.axis_index("dp")
    count = lax.axis_size("dp")
    whole = jnp.zeros((count * share, groups[0][0].shape[1]), groups[0][0].dtype)
    for array, offsets in groups:
        for n, k in enumerate(offsets):
            part = array[n * share : (n + 1) * share]
            whole = lax.dynamic_update_slice(whole, part, ((me ^ k) * share, 0))
    return [(whole, [])]


def arrays_of(groups):
    return [array for array, _ in groups]


def offsets_of(groups):
    return [offsets for _, offsets in groups]


def row_copies(me, shards, offsets, low, size, target, column, sem):
    copies = []
    columns, place = pl.ds(low, size), pl.ds(column, size)
    for shard, from_devices in zip(shards, offsets):
        if not from_devices:
            copies.append(
                pltpu.make_async_copy(shard.at[:, columns], target.at[:, place], sem)
            )
        for n, k in enumerate(from_devices):
            share = shard.shape[0] // len(from_devices)
            rows = pl.ds(pl.multiple_of((me ^ k) * share, 16), share)
            source = shard.at[pl.ds(n * share, share), columns]
            copies.append(pltpu.make_async_copy(source, target.at[rows, place], sem))
    return copies


def start_all(copies):
    for copy in copies:
        copy.start()


def wait_all(copies):
    for copy in copies:
        copy.wait()


def call(kernel, name, out_shape, operands, scratch):
    spaces = {
        "s": pl.BlockSpec(memory_space=pltpu.SMEM),
        "v": pl.BlockSpec(memory_space=pltpu.VMEM),
        "h": pl.BlockSpec(memory_space=pl.ANY),
    }
    return pl.pallas_call(
        kernel,
        out_shape=out_shape,
        in_specs=[spaces[space] for _, space in operands],
        out_specs=tuple(spaces["v"] for _ in out_shape),
        scratch_shapes=scratch,
        compiler_params=pltpu.CompilerParams(vmem_limit_bytes=VMEM_BYTES),
        cost_estimate=pl.CostEstimate(flops=1, transcendentals=0, bytes_accessed=1),
        name=name,
    )(*[array for array, _ in operands])


def shaped(rows, columns, kind=BF):
    return jax.ShapeDtypeStruct((rows, columns), kind)


def project(info, tokens, cosine, sine_tab, contexts):
    rows, width = tokens.shape
    block = min(rows, TILE)
    shards, offsets = arrays_of(contexts), offsets_of(contexts)
    wide = shards[0].shape[1]

    def kernel(info_ref, x_ref, cos_ref, sin_ref, *refs):
        shard_refs, refs = refs[: len(shards)], refs[len(shards) :]
        normed_ref, key_ref, value_ref, gain_ref, w_c, sems = refs
        copies = row_copies(info_ref[0], shard_refs, offsets, 0, wide, w_c, 0, sems.at[0])
        start_all(copies)
        wait_all(copies)
        terms = w_c[:, 2 * HD : 2 * HD + LANES].astype(F32).T
        gains = terms[0:2] + terms[2:4] + terms[4:6]
        gain_ref[...] = jnp.concatenate([gains] * 4, axis=0)
        for r in range(0, rows, block):
            span = pl.ds(r, block)
            x = x_ref[span, :].astype(F32)
            normed = (x * inverse_rms(x) * gains[0:1]).astype(BF)
            normed_ref[span, :] = normed
            raw = mm(normed, w_c[:, : 2 * HD], ((1,), (0,)))
            key_ref[span, :] = rotate(raw[:, :HD], cos_ref[span, :], sin_ref[span, :]).astype(BF)
            value_ref[span, :] = raw[:, HD:].astype(BF)

    return call(
        kernel,
        "project",
        (shaped(rows, width), *[shaped(rows, HD)] * 2, shaped(8, width, F32)),
        [(info, "s"), (tokens, "v"), (cosine, "v"), (sine_tab, "v")]
        + [(shard, "h") for shard in shards],
        [pltpu.VMEM((width, wide), BF), pltpu.SemaphoreType.DMA((1,))],
    )


def masked_scores(info_ref, query, keys):
    scores = mm(query, keys, ((1,), (1,))) * 0.0625
    at_row = info_ref[1] + lax.broadcasted_iota(jnp.int32, scores.shape, 0)
    at_key = lax.broadcasted_iota(jnp.int32, scores.shape, 1)
    allowed = (at_key <= at_row) & (at_key < info_ref[2])
    return jnp.where(allowed, scores, -1e30)


def attend(info, normed_own, keys, values, tokens_own, tables, gains, w_queries, w_outputs):
    own, width = tokens_own.shape
    q_shards, q_offsets = arrays_of(w_queries), offsets_of(w_queries)
    o_shards, o_offsets = arrays_of(w_outputs), offsets_of(w_outputs)
    across = q_shards[0].shape[1]

    def kernel(info_ref, own_ref, key_ref, value_ref, x_ref, cos_ref, sin_ref, gain_ref, *refs):
        q_refs, refs = refs[: len(q_shards)], refs[len(q_shards) :]
        o_refs, refs = refs[: len(o_shards)], refs[len(o_shards) :]
        query_ref, mixed_ref, middle_ref, normed_ref, log_ref, w_q, w_o, sems = refs
        copies = row_copies(info_ref[0], q_refs, q_offsets, 0, across, w_q, 0, sems.at[0])
        copies_o = row_copies(info_ref[0], o_refs, o_offsets, 0, across, w_o, 0, sems.at[1])
        start_all(copies)
        start_all(copies_o)
        wait_all(copies)
        keys, values = key_ref[...], value_ref[...]
        raw = mm(own_ref[...], w_q[...], ((1,), (0,)))
        for h in range(across // HD):
            columns = slice(h * HD, (h + 1) * HD)
            query = rotate(raw[:, columns], cos_ref[...], sin_ref[...]).astype(BF)
            query_ref[:, columns] = query
            scores = masked_scores(info_ref, query, keys)
            highest = jnp.max(scores, axis=-1, keepdims=True)
            exped = jnp.exp(scores - highest)
            total = jnp.sum(exped, axis=-1, keepdims=True)
            probs = (exped * (1.0 / total)).astype(BF)
            mixed_ref[:, columns] = mm(probs, values, ((1,), (0,))).astype(BF)
            log_ref[:, h : h + 1] = highest + jnp.log(total)
        wait_all(copies_o)
        middle = x_ref[...].astype(F32) + mm(mixed_ref[...], w_o[...], ((1,), (1,)))
        middle_ref[...] = middle
        normed_ref[...] = (middle * inverse_rms(middle) * gain_ref[1:2, :]).astype(BF)

    return call(
        kernel,
        "attend",
        (
            shaped(own, across),
            shaped(own, across),
            shaped(own, width, F32),
            shaped(own, width),
            shaped(own, LANES, F32),
        ),
        [(info, "s")]
        + [(array, "v") for array in (normed_own, keys, values, tokens_own, *tables, gains)]
        + [(shard, "h") for shard in q_shards + o_shards],
        [pltpu.VMEM((width, across), BF)] * 2 + [pltpu.SemaphoreType.DMA((2,))],
    )


def attend_back(
    info, parts, middle, grad_own, gains, queries, keys, values, log_sums, tables, w_outputs
):
    heads, n_parts = queries.shape[1] // HD, len(parts)
    own, width = middle.shape
    rows = keys.shape[0]
    output_shards, offsets = arrays_of(w_outputs), offsets_of(w_outputs)
    count = len(output_shards)

    def kernel(info_ref, *refs):
        part_refs, refs = refs[:n_parts], refs[n_parts:]
        middle_ref, grad_ref, gain_ref = refs[:3]
        query_ref, refs = refs[3], refs[4:]
        key_ref, value_ref, log_ref, cos_ref, sin_ref, cos_own, sin_own = refs[:7]
        shards, refs = refs[7 : 7 + count], refs[7 + count :]
        grad_middle_ref, low_ref, gain_two_ref, query_out, context_out, w_o, sem = refs
        copies = row_copies(info_ref[0], shards, offsets, 0, heads * HD, w_o, 0, sem.at[0])
        start_all(copies)
        grad_in = part_refs[0][...]
        for part_ref in part_refs[1:]:
            grad_in = grad_in + part_ref[...].astype(F32)
        middle = middle_ref[...]
        inverse = inverse_rms(middle)
        unit = middle * inverse
        gain_two = jnp.sum(grad_in * unit, axis=0, keepdims=True)
        gain_two_ref[...] = jnp.broadcast_to(gain_two, gain_two_ref.shape)
        grad_middle = grad_ref[...].astype(F32) + norm_back(
            grad_in, unit, inverse, gain_ref[1:2, :]
        )
        grad_middle_ref[...] = grad_middle
        low = grad_middle.astype(BF)
        low_ref[...] = low
        wait_all(copies)
        keys, values = key_ref[...], value_ref[...]
        grad_mixed = mm(low, w_o[...], ((1,), (0,))).astype(BF)
        grad_keys = grad_values = None
        for h in range(heads):
            query = query_ref[:, h * HD : (h + 1) * HD]
            scores = masked_scores(info_ref, query, keys)
            probs = jnp.exp(scores - log_ref[:, h : h + 1])
            grad_head = grad_mixed[:, h * HD : (h + 1) * HD]
            grad_probs = mm(grad_head, values, ((1,), (1,)))
            inner = jnp.sum(probs * grad_probs, axis=-1, keepdims=True)
            grad_scores = (probs * (grad_probs - inner)).astype(BF)
            turned = mm(grad_scores, keys, ((1,), (0,))) * 0.0625
            query_out[:, h * HD : (h + 1) * HD] = rotate(
                turned, cos_own[...], -sin_own[...]
            ).astype(BF)
            term_keys = mm(grad_scores, query, ((0,), (0,)))
            term_values = mm(probs.astype(BF), grad_head, ((0,), (0,)))
            grad_keys = term_keys if h == 0 else grad_keys + term_keys
            grad_values = term_values if h == 0 else grad_values + term_values
        context_out[:, :HD] = rotate(grad_keys * 0.0625, cos_ref[...], -sin_ref[...]).astype(BF)
        context_out[:, HD:] = grad_values.astype(BF)

    return call(
        kernel,
        "attend_back",
        (
            shaped(own, width, F32),
            shaped(own, width),
            shaped(8, width, F32),
            shaped(own, heads * HD),
            shaped(rows, 2 * HD),
        ),
        [(info, "s")]
        + [(part, "v") for part in parts]
        + [(middle, "v"), (grad_own, "v"), (gains, "v"), (queries, "v")]
        + [(array, "v") for array in (keys, values, log_sums, *tables)]
        + [(shard, "h") for shard in output_shards],
        [pltpu.VMEM((width, heads * HD), BF), pltpu.SemaphoreType.DMA((1,))],
    )


def store_sides(side, value, made, column, keep_ref, send_ref):
    blocks, share, _ = keep_ref.shape
    size = value.shape[1]
    for b in range(2 * blocks):
        made[b // 2, b % 2, :, :size] = value[b * share : (b + 1) * share].astype(BF)
    for b in range(blocks):
        keep_ref[b, :, column : column + size] = made[b, side, :, :size]
        send_ref[b, :, column : column + size] = made[b, 1 - side, :, :size]


def mixer_grads(
    info, normed, normed_own, grad_query, grad_context, low, mixed, gain_two, w_shards
):
    query_shards, context_shards = (arrays_of(groups) for groups in w_shards)
    offsets_q, offsets_c = (offsets_of(groups) for groups in w_shards)
    width = normed.shape[1]
    dp = lax.axis_size("dp")
    share = width // dp
    across = grad_query.shape[1]
    count = len(query_shards)
    first = jax.ShapeDtypeStruct((dp // 2, share, across + HD + LANES), BF)
    second = jax.ShapeDtypeStruct((dp // 2, share, across + HD), BF)

    def kernel(info_ref, *refs):
        normed_ref, own_ref, query_ref, context_ref, low_ref, mixed_ref, gain_ref = refs[:7]
        queries, contexts = refs[7 : 7 + count], refs[7 + count : 7 + 2 * count]
        keep_a, send_a, keep_b, send_b, w_q, w_c, made, sems = refs[7 + 2 * count :]
        side = info_ref[3]
        copies = row_copies(info_ref[0], queries, offsets_q, 0, across, w_q, 0, sems.at[0])
        copies_c = row_copies(info_ref[0], contexts, offsets_c, 0, 2 * HD, w_c, 0, sems.at[1])
        start_all(copies)
        start_all(copies_c)
        d_output = mm(low_ref[...], mixed_ref[...], ((0,), (0,)))
        halfway = across // HD // 2
        for h in range(across // HD):
            keep, send = (keep_a, send_a) if h < halfway else (keep_b, send_b)
            at = (2 * (h % halfway) + 1) * HD
            store_sides(side, d_output[:, h * HD : (h + 1) * HD], made, at, keep, send)
        d_query = mm(own_ref[...], query_ref[...], ((0,), (0,)))
        for h in range(across // HD):
            keep, send = (keep_a, send_a) if h < halfway else (keep_b, send_b)
            at = 2 * (h % halfway) * HD
            store_sides(side, d_query[:, h * HD : (h + 1) * HD], made, at, keep, send)
        d_context = mm(normed_ref[...], context_ref[...], ((0,), (0,)))
        store_sides(side, d_context[:, :HD], made, across, keep_a, send_a)
        store_sides(side, d_context[:, HD:], made, across, keep_b, send_b)
        wait_all(copies)
        wait_all(copies_c)
        gain_one = jnp.sum(d_query * w_q[...].astype(F32), axis=1, keepdims=True) + jnp.sum(
            d_context * w_c[...].astype(F32), axis=1, keepdims=True
        )
        second_gain = gain_ref[...].T
        lane = lax.broadcasted_iota(jnp.int32, (width, LANES), 1)
        both = jnp.where(lane == 0, gain_one, jnp.where(lane == 1, second_gain[:, 0:1], 0.0))
        store_sides(side, both, made, across + HD, keep_a, send_a)

    return call(
        kernel,
        "mixer_grads",
        (first, first, second, second),
        [(info, "s")]
        + [
            (array, "v")
            for array in (normed, normed_own, grad_query, grad_context, low, mixed, gain_two)
        ]
        + [(shard, "h") for shard in query_shards + context_shards],
        [
            pltpu.VMEM((width, across), BF),
            pltpu.VMEM((width, 2 * HD), BF),
            pltpu.VMEM((dp // 2, 2, share, across), BF),
            pltpu.SemaphoreType.DMA((2,)),
        ],
    )


def finish(info, grad_query, parts, grad_middle, tokens_own, gains, w_shards):
    query_shards, context_shards = (arrays_of(groups) for groups in w_shards)
    offsets_q, offsets_c = (offsets_of(groups) for groups in w_shards)
    own, width = grad_middle.shape
    across = grad_query.shape[1]
    count, n_parts = len(query_shards), len(parts)

    def kernel(info_ref, query_ref, *refs):
        part_refs, refs = refs[:n_parts], refs[n_parts:]
        middle_ref, x_ref, gain_ref = refs[:3]
        queries, contexts = refs[3 : 3 + count], refs[3 + count : 3 + 2 * count]
        out_ref, w_q, w_c, sems = refs[3 + 2 * count :]
        copies = row_copies(info_ref[0], queries, offsets_q, 0, across, w_q, 0, sems.at[0])
        copies_c = row_copies(info_ref[0], contexts, offsets_c, 0, 2 * HD, w_c, 0, sems.at[1])
        start_all(copies)
        start_all(copies_c)
        total = part_refs[0][...].astype(F32)
        for part_ref in part_refs[1:]:
            total = total + part_ref[...].astype(F32)
        x = x_ref[...].astype(F32)
        inverse = inverse_rms(x)
        wait_all(copies)
        wait_all(copies_c)
        grad_in = mm(query_ref[...], w_q[...], ((1,), (1,))) + mm(
            total.astype(BF), w_c[...], ((1,), (1,))
        )
        out_ref[...] = middle_ref[...] + norm_back(grad_in, x * inverse, inverse, gain_ref[0:1, :])

    return call(
        kernel,
        "finish",
        (shaped(own, width, F32),),
        [(info, "s"), (grad_query, "v")]
        + [(part, "v") for part in parts]
        + [(grad_middle, "v"), (tokens_own, "v"), (gains, "v")]
        + [(shard, "h") for shard in query_shards + context_shards],
        [
            pltpu.VMEM((width, across), BF),
            pltpu.VMEM((width, 2 * HD), BF),
            pltpu.SemaphoreType.DMA((2,)),
        ],
    )[0]


def feed_block(info, x, g, groups_a, groups_b, width, out_type):
    rows, depth = x.shape
    shards_a, shards_b = arrays_of(groups_a), arrays_of(groups_b)
    offsets, offsets_b = offsets_of(groups_a), offsets_of(groups_b)
    count = len(shards_a)
    half, cuts = column_cuts(width)

    def kernel(info_ref, x_ref, g_ref, *refs):
        first, second = refs[:count], refs[count : 2 * count]
        hid_ref, gate_ref, up_ref, feed_ref, back_ref = refs[2 * count : 2 * count + 5]
        w_gate, w_up, w_down, sems = refs[2 * count + 5 :]
        copies = []
        for n, (low, high) in enumerate(cuts):
            size = high - low
            source, at = (first, width + low) if high <= half else (second, width + low - half)
            group = []
            for shards, start, target in (
                (first, low, w_gate),
                (second, low, w_up),
                (source, at, w_down),
            ):
                own_offsets = offsets_b if shards is second else offsets
                group += row_copies(
                    info_ref[0], shards, own_offsets, start, size, target, low, sems.at[n]
                )
            copies.append(group)
            start_all(group)
        scale = 0.7978845608028654
        feed = back = None
        for n, (low, high) in enumerate(cuts):
            wait_all(copies[n])
            x, g = x_ref[...], g_ref[...]
            gate_w, up_w, down_w = w_gate[:, low:high], w_up[:, low:high], w_down[:, low:high]
            gate = mm(x, gate_w, ((1,), (0,)))
            up = mm(x, up_w, ((1,), (0,)))
            grad = mm(g, down_w, ((1,), (0,)))
            square = gate * gate
            tanh = jnp.tanh(scale * gate * (1.0 + 0.044715 * square))
            right = 0.5 * (1.0 + tanh)
            gelu = gate * right
            slope = right + gelu * (1.0 - tanh) * scale * (1.0 + 3 * 0.044715 * square)
            hidden = (gelu * up).astype(BF)
            grad_gate = (grad * up * slope).astype(BF)
            grad_up = (grad * gelu).astype(BF)
            hid_ref[:, low:high] = hidden
            gate_ref[:, low:high] = grad_gate
            up_ref[:, low:high] = grad_up
            feed_n = mm(hidden, down_w, ((1,), (1,)))
            back_n = mm(grad_gate, gate_w, ((1,), (1,))) + mm(grad_up, up_w, ((1,), (1,)))
            feed = feed_n if feed is None else feed + feed_n
            back = back_n if back is None else back + back_n
        feed_ref[...] = feed.astype(feed_ref.dtype)
        back_ref[...] = back.astype(back_ref.dtype)

    return call(
        kernel,
        "feed_block",
        (*[shaped(rows, width)] * 3, *[shaped(rows, depth, out_type)] * 2),
        [(info, "s"), (x, "v"), (g, "v")] + [(shard, "h") for shard in shards_a + shards_b],
        [pltpu.VMEM((depth, width), BF)] * 3 + [pltpu.SemaphoreType.DMA((3,))],
    )


def feed_grads(info, lefts, rights, low, high, firsts, whole):
    parts, dp = len(lefts), lax.axis_size("dp")
    depth, width = lefts[0].shape
    share = width // dp
    full = whole[0].shape[1]
    n_whole, n_part = full // TILE, (high - low) // TILE
    half = jax.ShapeDtypeStruct((dp // 2, share, full + high - low), BF)

    def kernel(info_ref, *refs):
        first_refs, whole_refs = refs[:parts], refs[parts : 2 * parts]
        left_refs, right_refs = refs[2 * parts : 3 * parts], refs[3 * parts : 4 * parts]
        keep_ref, send_ref, made = refs[4 * parts :]

        def one(rows, columns):
            total = None
            for row, column in zip(rows, columns):
                term = mm(row[...], column[...], ((0,), (0,)))
                total = term if total is None else total + term
            store_sides(info_ref[3], total, made, 0, keep_ref, send_ref)

        @pl.when(pl.program_id(0) < n_whole)
        def _():
            one(first_refs, whole_refs)

        @pl.when(pl.program_id(0) >= n_whole)
        def _():
            one(left_refs, right_refs)

    def whole_map(f, info_ref):
        return (0, jnp.minimum(f, n_whole - 1))

    def part_map(f, info_ref):
        return (0, low // TILE + jnp.maximum(f - n_whole, 0))

    fixed = pl.BlockSpec((depth, width), lambda f, info_ref: (0, 0))
    return pl.pallas_call(
        kernel,
        out_shape=(half, half),
        grid_spec=pltpu.PrefetchScalarGridSpec(
            num_scalar_prefetch=1,
            grid=(n_whole + n_part,),
            in_specs=[fixed] * parts
            + [pl.BlockSpec((depth, TILE), whole_map)] * parts
            + [fixed] * parts
            + [pl.BlockSpec((depth, TILE), part_map)] * parts,
            out_specs=[pl.BlockSpec((dp // 2, share, TILE), lambda f, info_ref: (0, 0, f))] * 2,
            scratch_shapes=[pltpu.VMEM((dp // 2, 2, share, TILE), BF)],
        ),
        compiler_params=pltpu.CompilerParams(vmem_limit_bytes=VMEM_BYTES),
        cost_estimate=pl.CostEstimate(flops=1, transcendentals=0, bytes_accessed=1),
        name="feed_grads",
    )(info, *firsts, *whole, *lefts, *rights)


class Halving:
    def __init__(self, keep, send, order):
        self.order = order
        self.left = [2**j for j in reversed(range(len(order)))]
        self.sent = swap(send, order[0])
        self.kept = keep
        self.left.remove(order[0])
        self.stage = 1

    def step(self):
        me = lax.axis_index("dp")
        total = (self.kept.astype(F32) + self.sent.astype(F32)).astype(BF)
        bit = self.order[self.stage]
        total = total.reshape((2,) * len(self.left) + total.shape[-2:])
        axis = self.left.index(bit)
        side = (me // bit) % 2
        self.kept = lax.dynamic_index_in_dim(total, side, axis, keepdims=False)
        self.sent = swap(lax.dynamic_index_in_dim(total, 1 - side, axis, keepdims=False), bit)
        self.left.remove(bit)
        self.stage += 1

    def done(self):
        while self.stage < len(self.order):
            self.step()
        return self.kept.astype(F32) + self.sent.astype(F32)


def after(values, *others):
    flat, tree = jax.tree.flatten((values, others))
    return jax.tree.unflatten(tree, lax.optimization_barrier(flat))


def local(
    tokens,
    cotangent,
    lengths,
    rates,
    query_weight,
    query_moment,
    query_average,
    output_weight,
    output_moment,
    output_average,
    gating_weight,
    gating_moment,
    gating_average,
    down_weight,
    down_moment,
    down_average,
    context_weight,
    context_moment,
    context_average,
    gains_weight,
    gains_moment,
    gains_average,
):
    row_count, width = tokens.shape
    dp, mp = lax.axis_size("dp"), lax.axis_size("mp")
    place = lax.axis_index("mp")
    own_count = row_count // mp
    own_start = place * own_count
    share, piece = width // dp, width // (dp * mp)
    forth, back = bit_orders()
    forth_first, back_first = forth[-1:] + forth[:-1], back[-1:] + back[:-1]
    length = lengths[0]
    places = jnp.arange(row_count, dtype=jnp.int32)
    me = lax.axis_index("dp")
    info = jnp.stack([me, own_start, length, me % 2]).astype(jnp.int32)

    def rows_at(tensor, step, count):
        return lax.dynamic_slice_in_dim(tensor, (place ^ step) * count, count, 0)

    gains_split = jnp.stack(split_three(gains_weight)).reshape(1, -1)
    message = jnp.concatenate(
        [
            query_weight.astype(BF),
            output_weight.T.astype(BF),
            context_weight.astype(BF).reshape(2 * piece, HD),
            jnp.pad(gains_split, ((0, 0), (0, HD - gains_split.shape[1]))),
        ],
        axis=0,
    )
    message = jnp.pad(message, ((0, -message.shape[0] % 16), (0, 0)))
    (gating_late, down_late), (message,) = after((gating_weight, down_weight), message)
    parts = [message] + [across_heads(message, k) for k in range(1, mp)]
    query_share = jnp.concatenate([part[:share] for part in parts], axis=1)
    output_share = jnp.concatenate([part[share : 2 * share] for part in parts], axis=1)
    rests = jnp.stack([part[2 * share :] for part in parts])
    rests = [lax.dynamic_index_in_dim(rests, place ^ k, 0, keepdims=False) for k in range(mp)]
    context_share = jnp.concatenate(
        [
            jnp.concatenate(
                [
                    rest[:piece],
                    rest[piece : 2 * piece],
                    jnp.pad(
                        rest[2 * piece, : 6 * piece].reshape(6, piece).T, ((0, 0), (0, LANES - 6))
                    ),
                ],
                axis=1,
            )
            for rest in rests
        ],
        axis=0,
    )

    units = gating_weight.shape[2]
    padded = round_up(units, TILE)
    half = column_cuts(padded)[0]

    def pad_units(tensor):
        return jnp.pad(tensor, ((0, 0), (0, padded - units)))

    gating_low = gating_late.astype(BF)
    down_low = pad_units(down_late.T.astype(BF))
    feed_a = jnp.concatenate([pad_units(gating_low[0]), down_low[:, :half]], axis=1)
    feed_b = jnp.concatenate([pad_units(gating_low[1]), down_low[:, half:]], axis=1)
    contexts = spread_direct(context_share)
    first_a, first_b = swap(feed_a, forth[0]), swap(feed_b, back[0])
    held_q, held_o = [query_share, swap(query_share, forth[0])], [output_share, swap(output_share, back[0])]

    cosine, sine_tab = rotation(row_count, HD)
    tokens_own = rows_at(tokens, 0, own_count)
    tables_own = (rows_at(cosine, 0, own_count), rows_at(sine_tab, 0, own_count))
    (cotangent_too, second_a, second_b), (context_held,) = after(
        (cotangent, feed_a, feed_b), contexts[0][0]
    )
    contexts = [(context_held, contexts[0][1])] + contexts[1:]
    grad_low = jnp.where((places < length)[:, None], cotangent_too, jnp.zeros_like(cotangent))
    grad_blocks = [rows_at(grad_low, k, own_count) for k in range(mp)]
    normed_one, (grad_blocks, tokens_own, tables_own, first_a, first_b) = after(
        contexts[1][0], grad_blocks, tokens_own, tables_own, first_a, first_b
    )
    contexts = [contexts[0], (normed_one, contexts[1][1])]
    contexts = lay(contexts)
    normed, keys, values, gains = project(info, tokens, cosine, sine_tab, contexts)
    normed_own = rows_at(normed, 0, own_count)
    (held_q, held_o), (gains,) = after((held_q, held_o), gains)
    w_queries = spread_on(held_q, forth)
    w_outputs = spread_on(held_o, back)
    (sent_a, sent_b), (w_queries[0], w_outputs[0]) = after(
        (first_a, first_b), w_queries[0], w_outputs[0]
    )
    w_queries, w_outputs = spread_out(w_queries, forth), spread_out(w_outputs, back)
    w_queries, w_outputs = lay(w_queries), lay(w_outputs)
    pieces_a, offsets_a = spread_wide([feed_a, first_a], [second_a, sent_a], forth)
    pieces_b, offsets_b = spread_wide([feed_b, first_b], [second_b, sent_b], back)
    shards_a = spread_last(pieces_a[:2], offsets_a[:2], forth[-1])
    shards_b = spread_last(pieces_b[:2], offsets_b[:2], back[-1])
    normed_own, (shards_a, shards_b) = after(
        normed_own, arrays_of(shards_a), arrays_of(shards_b)
    )
    shards_a = list(zip(shards_a, [offsets_a[:2], [k ^ 1 for k in offsets_a[:2]]]))
    shards_b = list(zip(shards_b, [offsets_b[:2], [k ^ 1 for k in offsets_b[:2]]]))
    queries, mixed, middle, normed_two_own, log_sums = attend(
        info, normed_own, keys, values, tokens_own, tables_own, gains, w_queries, w_outputs
    )

    (pieces_a[2:], pieces_b[2:]), (normed_two_own,) = after(
        (pieces_a[2:], pieces_b[2:]), normed_two_own
    )
    for n in range(2, len(pieces_a), 2):
        shards_a = shards_a + spread_last(pieces_a[n : n + 2], offsets_a[n : n + 2], forth[-1])
        shards_b = shards_b + spread_last(pieces_b[n : n + 2], offsets_b[n : n + 2], back[-1])
    shards_a, shards_b = lay(shards_a), lay(shards_b)
    blocks = [normed_two_own] + [across_heads(normed_two_own, k) for k in range(1, mp)]
    made = []
    for k in range(mp):
        if k > 0:
            blocks[k], (made[k - 1],) = after(blocks[k], made[k - 1])
        made.append(
            feed_block(
                info, blocks[k], grad_blocks[k], shards_a, shards_b, padded, F32 if k == 0 else BF
            )
        )
    hidden, grad_gate, grad_up, feed_parts, back_parts = (
        [made[k][n] for k in range(mp)] for n in range(5)
    )
    back_parts = back_parts[:1] + [across_heads(back_parts[k], k) for k in range(1, mp)]
    def halve(parts):
        rows, bit = parts[0].shape[0], mp // len(parts)
        sent = across_heads(jnp.concatenate(parts[1::2], axis=0), bit)
        return parts[0::2], [sent[k * rows : (k + 1) * rows] for k in range(len(parts) // 2)]

    def summed(kept, sent):
        return [a.astype(F32) + b.astype(F32) for a, b in zip(kept, sent)]

    def to_owner(parts):
        while len(parts) > 1:
            parts = summed(*halve([part.astype(BF) for part in parts]))
        return parts[0]

    keep_b, send_b = feed_grads(info, grad_blocks, hidden, half, padded, blocks, grad_up)
    send_b, (back_parts[:-1],) = after(send_b, back_parts[:-1])
    flow_b = Halving(keep_b, send_b, back_first)
    flow_b.step()
    grad_gate, (flow_b.kept,) = after(grad_gate, flow_b.kept)
    keep_a, send_a = feed_grads(info, grad_blocks, hidden, 0, half, blocks, grad_gate)
    send_a, (back_parts[-1],) = after(send_a, back_parts[-1])
    flow_a = Halving(keep_a, send_a, forth_first)
    flow_a.step()
    feed_parts, (back_parts,) = after(feed_parts, back_parts)
    feed_kept, feed_sent = halve([part.astype(BF) for part in feed_parts])
    back_parts, (flow_a.kept,) = after(back_parts, flow_a.kept)

    grad_middle, middle_low, gain_two, grad_query, grad_context = attend_back(
        info,
        back_parts,
        middle,
        grad_blocks[0],
        gains,
        queries,
        keys,
        values,
        log_sums,
        (cosine, sine_tab, *tables_own),
        w_outputs,
    )

    context_kept, context_sent = halve([rows_at(grad_context, k, own_count) for k in range(mp)])
    grad_query, (flow_b.sent,) = after(grad_query, flow_b.sent)
    w_shards = (w_queries, contexts)
    keep_a, send_a, keep_b, send_b = mixer_grads(
        info, normed, normed_own, grad_query, grad_context, middle_low, mixed, gain_two, w_shards
    )
    (send_a, send_b), (flow_a.sent,) = after((send_a, send_b), flow_a.sent)
    context_sent, (keep_a,) = after(context_sent, keep_a)
    context_own = to_owner(summed(context_kept, context_sent))
    mixer_a, mixer_b = Halving(keep_a, send_a, forth_first), Halving(keep_b, send_b, back_first)
    flow_a.step()
    flow_b.step()
    (mixer_a.sent, mixer_b.sent), (flow_a.kept, flow_b.kept) = after(
        (mixer_a.sent, mixer_b.sent), flow_a.kept, flow_b.kept
    )
    mixer_a.step()
    mixer_b.step()
    context_own, (mixer_a.kept, mixer_b.kept) = after(context_own, mixer_a.kept, mixer_b.kept)
    tokens_grad = finish(info, grad_query, [context_own], grad_middle, tokens_own, gains, w_shards)
    feed_sent, (mixer_a.sent, mixer_b.sent) = after(feed_sent, mixer_a.sent, mixer_b.sent)
    block_out = middle + to_owner(summed(feed_kept, feed_sent))

    feed_one, feed_two = flow_a.done(), flow_b.done()
    mixer_one, mixer_two = mixer_a.done(), mixer_b.done()
    across, halfway = grad_query.shape[1], mp // 2
    shares = [
        (mixer_one if k < halfway else mixer_two)[
            :, (k % halfway) * 2 * HD : (k % halfway + 1) * 2 * HD
        ]
        for k in range(mp)
    ]
    share_context = jnp.concatenate([mixer_one[:, across:], mixer_two[:, across:]], axis=1)
    wide = share_context.shape[1]
    total, sum_context = shares[0], rows_at(share_context, 0, piece)
    for k in range(1, mp):
        total = total + across_heads(shares[k].astype(BF), k).astype(F32)
        sent = across_heads(rows_at(share_context, k, piece).astype(BF), k)
        sum_context = sum_context + sent.astype(F32)
    sum_query, sum_output = total[:, :HD], total[:, HD:].T
    sum_gains = jnp.stack([sum_context[:, HD] / gains_weight[0], sum_context[:, HD + 1]])
    sum_context = jnp.stack([sum_context[:, :HD], sum_context[:, wide - HD :]])
    sum_gating = jnp.stack([feed_one[:, :units], feed_two[:, :units]])
    sum_down = jnp.concatenate([feed_one[:, padded:], feed_two[:, padded:]], axis=1)[:, :units].T

    query_grads, query_moments, query_averages, query_updated = advance(
        sum_query, query_moment, query_average, query_weight, rates[0]
    )
    output_grads, output_moments, output_averages, output_updated = advance(
        sum_output, output_moment, output_average, output_weight, rates[1]
    )
    gating_grads, gating_moments, gating_averages, gating_updated = advance(
        sum_gating, gating_moment, gating_average, gating_weight, rates[2]
    )
    down_grads, down_moments, down_averages, down_updated = advance(
        sum_down, down_moment, down_average, down_weight, rates[3]
    )
    context_grads, context_moments, context_averages, context_updated = advance(
        sum_context, context_moment, context_average, context_weight, rates[4]
    )
    gains_grads, gains_moments, gains_averages, gains_updated = advance(
        sum_gains, gains_moment, gains_average, gains_weight, rates[5]
    )
    return (
        block_out,
        tokens_grad,
        query_grads,
        query_moments,
        query_averages,
        query_updated,
        output_grads,
        output_moments,
        output_averages,
        output_updated,
        gating_grads,
        gating_moments,
        gating_averages,
        gating_updated,
        down_grads,
        down_moments,
        down_averages,
        down_updated,
        context_grads,
        context_moments,
        context_averages,
        context_updated,
        gains_grads,
        gains_moments,
        gains_averages,
        gains_updated,
    )


def solution(mesh):
    return jax.shard_map(
        local,
        mesh=mesh,
        in_specs=(
            P("dp", None),
            P("dp", None),
            P("dp"),
            P(),
            P("dp", "mp"),
            P("dp", "mp"),
            P("dp", "mp"),
            P("mp", "dp"),
            P("mp", "dp"),
            P("mp", "dp"),
            P(None, "dp", "mp"),
            P(None, "dp", "mp"),
            P(None, "dp", "mp"),
            P("mp", "dp"),
            P("mp", "dp"),
            P("mp", "dp"),
            P(None, ("dp", "mp"), None),
            P(None, ("dp", "mp"), None),
            P(None, ("dp", "mp"), None),
            P(None, ("dp", "mp")),
            P(None, ("dp", "mp")),
            P(None, ("dp", "mp")),
        ),
        out_specs=(
            P(("dp", "mp"), None),
            P(("dp", "mp"), None),
            P("dp", "mp"),
            P("dp", "mp"),
            P("dp", "mp"),
            P("dp", "mp"),
            P("mp", "dp"),
            P("mp", "dp"),
            P("mp", "dp"),
            P("mp", "dp"),
            P(None, "dp", "mp"),
            P(None, "dp", "mp"),
            P(None, "dp", "mp"),
            P(None, "dp", "mp"),
            P("mp", "dp"),
            P("mp", "dp"),
            P("mp", "dp"),
            P("mp", "dp"),
            P(None, ("dp", "mp"), None),
            P(None, ("dp", "mp"), None),
            P(None, ("dp", "mp"), None),
            P(None, ("dp", "mp"), None),
            P(None, ("dp", "mp")),
            P(None, ("dp", "mp")),
            P(None, ("dp", "mp")),
            P(None, ("dp", "mp")),
        ),
        check_vma=False,
    )
```

time: 631 us -> 404 us (0.64)
  Pallas kernels: 0 us -> 125 us
  matrix products: 113 us -> 0 us
  local copies, waits for them, and re-layouts: 132 us -> 40.8 us
  waiting for transfers between devices: 193 us -> 132 us
  starting transfers between devices: 113 us -> 52.6 us
  other arithmetic: 69.8 us -> 45.5 us
    pallas_call x0 -> x11, Pallas kernels: none -> 125 us  [the longest x9 92.6 us: call(): pl.pallas_call(kernel, out_shape=out_shape, in_specs=[spaces[space] for _...]
    dot_general x24 -> x0, matrix products: 113 us -> none  [the longest x18 107 us: mm(): return lax.dot_general(a, b, (dims, ((), ())), preferred_element_type=F32)]
    ppermute x80 -> x32, waiting for transfers between devices: 126 us -> 64.8 us  [swap(): return lax.ppermute(tensor, 'dp', [(i, i ^ bit) for i in range(count)])]
    ppermute x30 -> x19, starting transfers between devices: 58.1 us -> 26.1 us  [across_heads(): return lax.ppermute(tensor, 'mp', [(i, i ^ bit) for i in range(count)])]
    ppermute x80 -> x32, starting transfers between devices: 54.4 us -> 26.5 us  [swap(): return lax.ppermute(tensor, 'dp', [(i, i ^ bit) for i in range(count)])]
    dynamic_update_slice x60 -> x0, local copies, waits for them, and re-layouts: 26.4 us -> none  [assemble(): whole = lax.dynamic_update_slice(whole, held[k], ((me ^ k) * share, column))]
    slice x14 -> x18, local copies, waits for them, and re-layouts: 18.3 us -> 2.25 us  [the longest x4 0.96 us: local(): part[share:2 * share]]
    convert_element_type x6 -> x1, local copies, waits for them, and re-layouts: 14.5 us -> 0.01 us  [local(): context_weight.astype(BF).reshape(2 * piece, HD)]
  transfers between devices with their start and end apart: 110 -> 51, of which waited for: 32 -> 22; matrix products, arithmetic and copies ran while one was open for 35% -> 16% of each run, Pallas kernels for 0% -> 31%
where the time goes in v2:
time: 404 us; the launch traced here: 398 us
  waiting for transfers between devices  132 us (33%)
  Pallas kernels  125 us (31%)
  starting transfers between devices  52.6 us (13%)
  other arithmetic  45.5 us (11%)
  local copies, waits for them, and re-layouts  40.8 us (10%)
    pallas_call x9, Pallas kernels, call(): pl.pallas_call(kernel, out_shape=out_shape, in_specs=[spaces[space] for _...  92.6 us
    ppermute x19, waiting for transfers between devices, across_heads(): return lax.ppermute(tensor, 'mp', [(i, i ^ bit) for i in range(count)])  66.8 us
    ppermute x32, waiting for transfers between devices, swap(): return lax.ppermute(tensor, 'dp', [(i, i ^ bit) for i in range(count)])  64.8 us
    pallas_call x2, Pallas kernels, feed_grads(): pl.pallas_call(kernel, out_shape=(half, half), grid_spec=pltpu.PrefetchSc...  31.9 us
    ppermute x32, starting transfers between devices, swap(): return lax.ppermute(tensor, 'dp', [(i, i ^ bit) for i in range(count)])  26.5 us
    ppermute x19, starting transfers between devices, across_heads(): return lax.ppermute(tensor, 'mp', [(i, i ^ bit) for i in range(count)])  26.1 us
    unnamed x116, local copies, waits for them, and re-layouts  17.5 us
    add x6, other arithmetic, advance(): average_new = AVERAGING * average + (1.0 - AVERAGING) * weight_new  12.3 us
  transfers between devices with their start and end apart: 51, of which 22 were waited for; matrix products, arithmetic and copies ran while one was open for 16% of the time, Pallas kernels for 31%

profile of v2, /device:TPU:0, one launch (start us, length us, event | category | flops | bytes accessed | tf_op | source)
XLA Modules:
  0.0 397.8 jit_solution(9188804012065893530)
XLA Ops:
  4.3 5.1 %collective-permute-start.2 = (bf16[368,256]{1,0:T(8,128)(2,1)S(1)}, bf16[368,256]{1,0:T(8,128)(2,1)S(1)}, u32[]{:S(2)}, u32[]{:S(2)}) collective-permute-start(bf16[368,256]{1,0:T(8,128)(2,1)S(1)} %pad.32), channel_id=1, source_target_pairs={{0,3},{1,2},{2,1},{3,0},{4,7},{5,6},{6,5},{7,4},{8,11},{9,10},{10,... | collective-permute-start | bytes 565256 | tf_op jit(solution)/shard_map/ppermute | solution.py:62
  10.1 1.7 convert_element_type.269
  14.0 1.6 collective-permute-start.7
  19.4 1.9 multiply_sine_fusion
  21.3 2.3 constant_dynamic-slice_fusion.5.x_ref.refs_2_
  34.4 4.8 %collective-permute-done.3 = bf16[144,640]{1,0:T(8,128)(2,1)S(1)} collective-permute-done((bf16[144,640]{1,0:T(8,128)(2,1)S(1)}, bf16[144,640]{1,0:T(8,128)(2,1)S(1)}, u32[]{:S(2)}, u32[]{:S(2)}) %collective-permute-start.3) | collective-permute-done | bytes 184352 | tf_op jit(solution)/shard_map/ppermute | solution.py:57
  40.8 2.6 collective-permute-start.12
  44.3 5.8 %concatenate.80.refs_0_.refs_9_.refs_6_ = bf16[576,640]{1,0:T(8,128)(2,1)S(1)} concatenate(bf16[36,640]{1,0:T(8,128)(2,1)} %pad_maximum_fusion.16, bf16[36,640]{1,0:T(8,128)(2,1)} %pad_maximum_fusion.17, bf16[36,640]{1,0:T(8,128)(2,1)} %pad_maximum_fusion.18, bf16[36,640]{1,0:T(8,128)(2,1)S(1)} %pad_maximum_fusion.19, bf16[144,640]{1,0:T(8,128)(2,1)} %copy-done.39, ...), dimensions={0} | concatenate | bytes 1474560 | tf_op jit(solution)/shard_map/concatenate | solution.py:97
  50.2 2.2 broadcast_select_fusion
  54.9 6.4 %project.1 = (bf16[1024,1152]{1,0:T(8,128)(2,1)}, bf16[1024,256]{1,0:T(8,128)(2,1)}, bf16[1024,256]{1,0:T(8,128)(2,1)}, f32[8,1152]{1,0:T(8,128)}) custom-call(s32[4]{0:T(128)} %pad_add_fusion.info_ref, bf16[1024,1152]{1,0:T(8,128)(2,1)} %x_ref.1, f32[1024,128]{1,0:T(8,128)} %copy-done.15, f32[1024,128]{1,0:T(8,128)} %copy-done.14, ...), custom_call_target="tpu_custom_call" | custom-call | flops 1 | bytes 1 | tf_op jit(solution)/shard_map/project/pallas_call | solution.py:179
  64.9 1.7 pad_maximum_fusion.2.refs_4_
  66.7 10.3 %collective-permute-done.14 = bf16[288,1024]{1,0:T(8,128)(2,1)S(1)} collective-permute-done((bf16[288,1024]{1,0:T(8,128)(2,1)S(1)}, bf16[288,1024]{1,0:T(8,128)(2,1)S(1)}, u32[]{:S(2)}, u32[]{:S(2)}) %collective-permute-start.14) | collective-permute-done | bytes 589856 | tf_op jit(solution)/shard_map/ppermute | solution.py:57
  84.1 1.9 constant_dynamic-slice_fusion.2.own_ref.refs_1_
  87.1 8.6 %attend.1 = (bf16[256,1024]{1,0:T(8,128)(2,1)}, bf16[256,1024]{1,0:T(8,128)(2,1)}, f32[256,1152]{1,0:T(8,128)}, bf16[256,1152]{1,0:T(8,128)(2,1)}, f32[256,128]{1,0:T(8,128)}) custom-call(s32[4]{0:T(128)} %pad_add_fusion.info_ref, bf16[256,1152]{1,0:T(8,128)(2,1)} %constant_dynamic-slice_fusion.2.own_ref.refs_1_, ...), custom_call_target="tpu_custom_call" | custom-call | flops 1 | bytes 1 | tf_op jit(solution)/shard_map/attend/pallas_call | solution.py:179
  95.7 5.1 %collective-permute-done.19 = bf16[144,2560]{1,0:T(8,128)(2,1)} collective-permute-done((bf16[144,2560]{1,0:T(8,128)(2,1)}, bf16[144,2560]{1,0:T(8,128)(2,1)}, u32[]{:S(2)}, u32[]{:S(2)}) %collective-permute-start.19) | collective-permute-done | bytes 737312 | tf_op jit(solution)/shard_map/ppermute | solution.py:57
  100.8 14.2 %collective-permute-done.20 = bf16[144,2560]{1,0:T(8,128)(2,1)S(1)} collective-permute-done((bf16[144,2560]{1,0:T(8,128)(2,1)}, bf16[144,2560]{1,0:T(8,128)(2,1)S(1)}, u32[]{:S(2)}, u32[]{:S(2)}) %collective-permute-start.20) | collective-permute-done | bytes 737312 | tf_op jit(solution)/shard_map/ppermute | solution.py:57
  114.9 1.7 collective-permute-done.18
  120.4 2.9 collective-permute-start.24
  125.9 13.0 %feed_block.4 = (bf16[256,1792]{1,0:T(8,128)(2,1)}, bf16[256,1792]{1,0:T(8,128)(2,1)}, bf16[256,1792]{1,0:T(8,128)(2,1)}, f32[256,1152]{1,0:T(8,128)}, f32[256,1152]{1,0:T(8,128)}) custom-call(s32[4]{0:T(128)} %pad_add_fusion.info_ref, bf16[256,1152]{1,0:T(8,128)(2,1)} %get-tuple-element.194.x_ref.refs_0_, ...), custom_call_target="tpu_custom_call" | custom-call | flops 1 | bytes 1 | tf_op jit(solution)/shard_map/feed_block/pallas_call | solution.py:179
  138.9 6.9 %collective-permute-done.21.x_ref.refs_1_ = bf16[256,1152]{1,0:T(8,128)(2,1)S(1)} collective-permute-done((bf16[256,1152]{1,0:T(8,128)(2,1)S(1)}, bf16[256,1152]{1,0:T(8,128)(2,1)S(1)}, u32[]{:S(2)}, u32[]{:S(2)}) %collective-permute-start.21) | collective-permute-done | bytes 589856 | tf_op jit(solution)/shard_map/ppermute | solution.py:62
  146.6 12.4 %feed_block.5 = (bf16[256,1792]{1,0:T(8,128)(2,1)}, bf16[256,1792]{1,0:T(8,128)(2,1)}, bf16[256,1792]{1,0:T(8,128)(2,1)}, bf16[256,1152]{1,0:T(8,128)(2,1)}, bf16[256,1152]{1,0:T(8,128)(2,1)}) custom-call(s32[4]{0:T(128)} %pad_add_fusion.info_ref, bf16[256,1152]{1,0:T(8,128)(2,1)} %copy-done.17, bf16[256,1152]{1,0:T(8,128)(2,1)} %get-tuple-element.211.g_ref.refs_9_, ...), custom_call_target="tpu_custom_call" | custom-call | flops 1 | bytes 1 | tf_op jit(solution)/shard_map/feed_block/pallas_call | solution.py:179
  159.1 3.7 collective-permute-done.24.x_ref.refs_2_
  163.6 12.8 %feed_block.6 = (bf16[256,1792]{1,0:T(8,128)(2,1)}, bf16[256,1792]{1,0:T(8,128)(2,1)}, bf16[256,1792]{1,0:T(8,128)(2,1)}, bf16[256,1152]{1,0:T(8,128)(2,1)}, bf16[256,1152]{1,0:T(8,128)(2,1)}) custom-call(s32[4]{0:T(128)} %pad_add_fusion.info_ref, bf16[256,1152]{1,0:T(8,128)(2,1)} %copy-done.18, bf16[256,1152]{1,0:T(8,128)(2,1)} %get-tuple-element.219.g_ref.refs_10_, ...), custom_call_target="tpu_custom_call" | custom-call | flops 1 | bytes 1 | tf_op jit(solution)/shard_map/feed_block/pallas_call | solution.py:179
  176.5 2.9 collective-permute-start.26
  179.4 12.4 %feed_block.7 = (bf16[256,1792]{1,0:T(8,128)(2,1)}, bf16[256,1792]{1,0:T(8,128)(2,1)}, bf16[256,1792]{1,0:T(8,128)(2,1)}, bf16[256,1152]{1,0:T(8,128)(2,1)}, bf16[256,1152]{1,0:T(8,128)(2,1)}) custom-call(s32[4]{0:T(128)} %pad_add_fusion.info_ref, bf16[256,1152]{1,0:T(8,128)(2,1)} %collective-permute-done.25.x_ref.refs_3_, ...), custom_call_target="tpu_custom_call" | custom-call | flops 1 | bytes 1 | tf_op jit(solution)/shard_map/feed_block/pallas_call | solution.py:179
  191.8 15.1 %feed_grads.2 = (bf16[4,144,2560]{2,1,0:T(8,128)(2,1)}, bf16[4,144,2560]{2,1,0:T(8,128)(2,1)}) custom-call(s32[4]{0:T(128)} %pad_add_fusion.info_ref, bf16[256,1152]{1,0:T(8,128)(2,1)} %get-tuple-element.194.x_ref.refs_0_, bf16[256,1152]{1,0:T(8,128)(2,1)} %copy-done.17, bf16[256,1152]{1,0:T(8,128)(2,1)} %copy-done.18, ...), custom_call_target="tpu_custom_call" | custom-call | flops 1 | bytes 1 | tf_op jit(solution)/shard_map/feed_grads/pallas_call | solution.py:578
  209.3 4.1 %collective-permute-done.28 = bf16[4,144,2560]{2,1,0:T(8,128)(2,1)S(1)} collective-permute-done((bf16[4,144,2560]{2,1,0:T(8,128)(2,1)}, bf16[4,144,2560]{2,1,0:T(8,128)(2,1)S(1)}, u32[]{:S(2)}, u32[]{:S(2)}) %collective-permute-start.28) | collective-permute-done | bytes 2949152 | tf_op jit(solution)/shard_map/ppermute | solution.py:57
  213.4 2.6 add_convert_fusion.1
  217.3 16.9 %feed_grads.3 = (bf16[4,144,2816]{2,1,0:T(8,128)(2,1)}, bf16[4,144,2816]{2,1,0:T(8,128)(2,1)}) custom-call(s32[4]{0:T(128)} %pad_add_fusion.info_ref, bf16[256,1152]{1,0:T(8,128)(2,1)} %get-tuple-element.194.x_ref.refs_0_, bf16[256,1152]{1,0:T(8,128)(2,1)} %copy-done.17, bf16[256,1152]{1,0:T(8,128)(2,1)} %copy-done.18, ...), custom_call_target="tpu_custom_call" | custom-call | flops 1 | bytes 1 | tf_op jit(solution)/shard_map/feed_grads/pallas_call | solution.py:578
  236.8 2.1 collective-permute-start.30
  240.4 3.7 add_convert_fusion
  246.0 19.3 %collective-permute-done.30 = bf16[512,1152]{1,0:T(8,128)(2,1)S(1)} collective-permute-done((bf16[512,1152]{1,0:T(8,128)(2,1)S(1)}, bf16[512,1152]{1,0:T(8,128)(2,1)S(1)}, u32[]{:S(2)}, u32[]{:S(2)}) %collective-permute-start.30) | collective-permute-done | bytes 1179680 | tf_op jit(solution)/shard_map/ppermute | solution.py:62
  265.4 11.0 %attend_back.1 = (f32[256,1152]{1,0:T(8,128)}, bf16[256,1152]{1,0:T(8,128)(2,1)}, f32[8,1152]{1,0:T(8,128)}, bf16[256,1024]{1,0:T(8,128)(2,1)}, bf16[1024,512]{1,0:T(8,128)(2,1)}) custom-call(s32[4]{0:T(128)} %pad_add_fusion.info_ref, f32[256,1152]{1,0:T(8,128)} %get-tuple-element.266.refs_0_, bf16[256,1152]{1,0:T(8,128)(2,1)} %copy-done.32, ...), custom_call_target="tpu_custom_call" | custom-call | flops 1 | bytes 1 | tf_op jit(solution)/shard_map/attend_back/pallas_call | solution.py:179
  278.3 1.7 collective-permute-start.32
  280.0 9.7 %mixer_grads.1 = (bf16[4,144,1408]{2,1,0:T(8,128)(2,1)}, bf16[4,144,1408]{2,1,0:T(8,128)(2,1)}, bf16[4,144,1280]{2,1,0:T(8,128)(2,1)}, bf16[4,144,1280]{2,1,0:T(8,128)(2,1)}) custom-call(s32[4]{0:T(128)} %pad_add_fusion.info_ref, bf16[1024,1152]{1,0:T(8,128)(2,1)} %get-tuple-element.171.refs_0_, ...), custom_call_target="tpu_custom_call" | custom-call | flops 1 | bytes 1 | tf_op jit(solution)/shard_map/mixer_grads/pallas_call | solution.py:179
  290.1 2.0 collective-permute-done.32
  295.1 11.0 %collective-permute-done.40 = bf16[256,512]{1,0:T(8,128)(2,1)S(1)} collective-permute-done((bf16[256,512]{1,0:T(8,128)(2,1)S(1)}, bf16[256,512]{1,0:T(8,128)(2,1)S(1)}, u32[]{:S(2)}, u32[]{:S(2)}) %collective-permute-start.40) | collective-permute-done | bytes 262176 | tf_op jit(solution)/shard_map/ppermute | solution.py:62
  306.9 1.8 add_convert_fusion.3
  315.0 14.9 %collective-permute-done.46 = bf16[144,2816]{1,0:T(8,128)(2,1)S(1)} collective-permute-done((bf16[144,2816]{1,0:T(8,128)(2,1)S(1)}, bf16[144,2816]{1,0:T(8,128)(2,1)S(1)}, u32[]{:S(2)}, u32[]{:S(2)}) %collective-permute-start.46) | collective-permute-done | bytes 811040 | tf_op jit(solution)/shard_map/ppermute | solution.py:57
  333.0 4.4 %add_multiply_fusion = (f32[2,144,1728]{2,1,0:T(8,128)}, f32[2,144,1728]{2,1,0:T(8,128)}, f32[2,144,1728]{2,1,0:T(8,128)}, f32[2,144,1728]{2,1,0:T(8,128)}) fusion(f32[2,144,1728]{2,1,0:T(8,128)S(1)} %copy-done.24, f32[2,144,1728]{2,1,0:T(8,128)S(1)} %copy-done.12, f32[]{:T(128)} %bitcast.56, f32[2,144,1728]{2,1,0:T(8,128)S(1)} %copy-done.25, ...), kind=kLoop, calls=%fused_computation.8 | loop fusion | flops 4478976 | bytes 15925252 | tf_op jit(solution)/shard_map/add | solution.py:51
  337.4 6.3 %finish.1 = f32[256,1152]{1,0:T(8,128)} custom-call(s32[4]{0:T(128)} %pad_add_fusion.info_ref, bf16[256,1024]{1,0:T(8,128)(2,1)} %get-tuple-element.274.refs_2_.query_ref, f32[256,512]{1,0:T(8,128)} %convert_add_fusion.4.refs_0_, f32[256,1152]{1,0:T(8,128)} %get-tuple-element.297.refs_1_, bf16[256,1152]{1,0:T(8,128)(2,1)} %constant_dynamic-slice_fusion.5.x_ref.refs_2_, ...), custom_call_target="tpu_custom_call" | custom-call | flops 1 | bytes 1 | tf_op jit(solution)/shard_map/finish/pallas_call | solution.py:179
  345.2 2.9 add_multiply_fusion.1
  352.1 4.9 %collective-permute-done.43 = bf16[144,1280]{1,0:T(8,128)(2,1)S(1)} collective-permute-done((bf16[144,1280]{1,0:T(8,128)(2,1)S(1)}, bf16[144,1280]{1,0:T(8,128)(2,1)S(1)}, u32[]{:S(2)}, u32[]{:S(2)}) %collective-permute-start.43) | collective-permute-done | bytes 368672 | tf_op jit(solution)/shard_map/ppermute | solution.py:57
  358.7 2.1 collective-permute-start.49
  360.8 2.3 collective-permute-start.50
  363.2 3.8 collective-permute-done.48
  368.5 17.4 %collective-permute-done.49 = bf16[36,640]{1,0:T(8,128)(2,1)S(1)} collective-permute-done((bf16[36,640]{1,0:T(8,128)(2,1)S(1)}, bf16[36,640]{1,0:T(8,128)(2,1)S(1)}, u32[]{:S(2)}, u32[]{:S(2)}) %collective-permute-start.49) | collective-permute-done | bytes 46112 | tf_op jit(solution)/shard_map/ppermute | solution.py:62
  390.9 2.3 collective-permute-done.42
  (301 shorter events, 88.2 us)
Async XLA Ops:
  4.3 20.6 %collective-permute-start.2 = (bf16[368,256]{1,0:T(8,128)(2,1)S(1)}, bf16[368,256]{1,0:T(8,128)(2,1)S(1)}, u32[]{:S(2)}, u32[]{:S(2)}) collective-permute-start(bf16[368,256]{1,0:T(8,128)(2,1)S(1)} %pad.32), channel_id=1, source_target_pairs={{0,3},{1,2},{2,1},{3,0},{4,7},{5,6},{6,5},{7,4},{8,11},{9,10},{10,... | collective-permute-start | bytes 565256 | tf_op jit(solution)/shard_map/ppermute | solution.py:62
  9.4 16.0 %collective-permute-start.1 = (bf16[368,256]{1,0:T(8,128)(2,1)S(1)}, bf16[368,256]{1,0:T(8,128)(2,1)S(1)}, u32[]{:S(2)}, u32[]{:S(2)}) collective-permute-start(bf16[368,256]{1,0:T(8,128)(2,1)S(1)} %pad.32), channel_id=1, source_target_pairs={{0,2},{1,3},{2,0},{3,1},{4,6},{5,7},{6,4},{7,5},{8,10},{9,11},{10,... | collective-permute-start | bytes 565256 | tf_op jit(solution)/shard_map/ppermute | solution.py:62
  9.4 16.0 %collective-permute-start = (bf16[368,256]{1,0:T(8,128)(2,1)S(1)}, bf16[368,256]{1,0:T(8,128)(2,1)S(1)}, u32[]{:S(2)}, u32[]{:S(2)}) collective-permute-start(bf16[368,256]{1,0:T(8,128)(2,1)S(1)} %pad.32), channel_id=1, source_target_pairs={{0,1},{1,0},{2,3},{3,2},{4,5},{5,4},{6,7},{7,6},{8,9},{9,8},{10,11... | collective-permute-start | bytes 565256 | tf_op jit(solution)/shard_map/ppermute | solution.py:62
  14.0 40.0 %collective-permute-start.7 = (bf16[144,2816]{1,0:T(8,128)(2,1)}, bf16[144,2816]{1,0:T(8,128)(2,1)}, u32[]{:S(2)}, u32[]{:S(2)}) collective-permute-start(bf16[144,2816]{1,0:T(8,128)(2,1)} %pad_maximum_fusion.7), channel_id=1, source_target_pairs={{0,8},{4,12},{8,0},{12,4},{16,24},{20,28},{24,16},{28,20},{1,9},{5... | collective-permute-start | bytes 2433032 | tf_op jit(solution)/shard_map/ppermute | solution.py:57
  16.6 37.3 %collective-permute-start.8 = (bf16[144,2560]{1,0:T(8,128)(2,1)}, bf16[144,2560]{1,0:T(8,128)(2,1)}, u32[]{:S(2)}, u32[]{:S(2)}) collective-permute-start(bf16[144,2560]{1,0:T(8,128)(2,1)} %pad_maximum_fusion.8), channel_id=1, source_target_pairs={{0,16},{4,20},{8,24},{12,28},{16,0},{20,4},{24,8},{28,12},{1,17},{... | collective-permute-start | bytes 2211848 | tf_op jit(solution)/shard_map/ppermute | solution.py:57
  27.9 11.3 %collective-permute-start.3 = (bf16[144,640]{1,0:T(8,128)(2,1)S(1)}, bf16[144,640]{1,0:T(8,128)(2,1)S(1)}, u32[]{:S(2)}, u32[]{:S(2)}) collective-permute-start(bf16[144,640]{1,0:T(8,128)(2,1)S(1)} %maximum_maximum_fusion), channel_id=1, source_target_pairs={{0,8},{4,12},{8,0},{12,4},{16,24},{20,28},{24,16},{28,20},{1,9},{5... | collective-permute-start | bytes 552968 | tf_op jit(solution)/shard_map/ppermute | solution.py:57
  29.4 11.4 %collective-permute-start.4 = (bf16[144,640]{1,0:T(8,128)(2,1)S(1)}, bf16[144,640]{1,0:T(8,128)(2,1)S(1)}, u32[]{:S(2)}, u32[]{:S(2)}) collective-permute-start(bf16[144,640]{1,0:T(8,128)(2,1)S(1)} %maximum_maximum_fusion), channel_id=1, source_target_pairs={{0,16},{4,20},{8,24},{12,28},{16,0},{20,4},{24,8},{28,12},{1,17},{... | collective-permute-start | bytes 552968 | tf_op jit(solution)/shard_map/ppermute | solution.py:57
  31.0 13.4 %collective-permute-start.5 = (bf16[144,640]{1,0:T(8,128)(2,1)S(1)}, bf16[144,640]{1,0:T(8,128)(2,1)}, u32[]{:S(2)}, u32[]{:S(2)}) collective-permute-start(bf16[144,640]{1,0:T(8,128)(2,1)S(1)} %maximum_maximum_fusion), channel_id=1, source_target_pairs={{0,24},{4,28},{8,16},{12,20},{16,8},{20,12},{24,0},{28,4},{1,25},{... | collective-permute-start | bytes 552968 | tf_op jit(solution)/shard_map/ppermute | solution.py:57
  39.2 22.1 %collective-permute-start.11 = (bf16[144,1024]{1,0:T(8,128)(2,1)S(1)}, bf16[144,1024]{1,0:T(8,128)(2,1)S(1)}, u32[]{:S(2)}, u32[]{:S(2)}) collective-permute-start(bf16[144,1024]{1,0:T(8,128)(2,1)S(1)} %pad_maximum_fusion.12), channel_id=1, source_target_pairs={{0,8},{4,12},{8,0},{12,4},{16,24},{20,28},{24,16},{28,20},{1,9},{5... | collective-permute-start | bytes 884744 | tf_op jit(solution)/shard_map/ppermute | solution.py:57
  40.8 20.5 %collective-permute-start.12 = (bf16[144,1024]{1,0:T(8,128)(2,1)S(1)}, bf16[144,1024]{1,0:T(8,128)(2,1)S(1)}, u32[]{:S(2)}, u32[]{:S(2)}) collective-permute-start(bf16[144,1024]{1,0:T(8,128)(2,1)S(1)} %pad_maximum_fusion.13), channel_id=1, source_target_pairs={{0,16},{4,20},{8,24},{12,28},{16,0},{20,4},{24,8},{28,12},{1,17},{... | collective-permute-start | bytes 884744 | tf_op jit(solution)/shard_map/ppermute | solution.py:57
  61.4 15.6 %collective-permute-start.14 = (bf16[288,1024]{1,0:T(8,128)(2,1)S(1)}, bf16[288,1024]{1,0:T(8,128)(2,1)S(1)}, u32[]{:S(2)}, u32[]{:S(2)}) collective-permute-start(bf16[288,1024]{1,0:T(8,128)(2,1)S(1)} %pad_maximum_fusion.10), channel_id=1, source_target_pairs={{0,8},{4,12},{8,0},{12,4},{16,24},{20,28},{24,16},{28,20},{1,9},{5... | collective-permute-start | bytes 1769480 | tf_op jit(solution)/shard_map/ppermute | solution.py:57
  63.0 15.3 %collective-permute-start.13 = (bf16[288,1024]{1,0:T(8,128)(2,1)S(1)}, bf16[288,1024]{1,0:T(8,128)(2,1)S(1)}, u32[]{:S(2)}, u32[]{:S(2)}) collective-permute-start(bf16[288,1024]{1,0:T(8,128)(2,1)S(1)} %pad_maximum_fusion.9), channel_id=1, source_target_pairs={{0,16},{4,20},{8,24},{12,28},{16,0},{20,4},{24,8},{28,12},{1,17},{... | collective-permute-start | bytes 1769480 | tf_op jit(solution)/shard_map/ppermute | solution.py:57
  64.8 16.2 %collective-permute-start.9 = (bf16[288,2816]{1,0:T(8,128)(2,1)S(1)}, bf16[288,2816]{1,0:T(8,128)(2,1)S(1)}, u32[]{:S(2)}, u32[]{:S(2)}) collective-permute-start(bf16[288,2816]{1,0:T(8,128)(2,1)S(1)} %pad_maximum_fusion.1.refs_0_), channel_id=1, source_target_pairs={{0,4},{4,0},{8,12},{12,8},{16,20},{20,16},{24,28},{28,24},{1,5},{5... | collective-permute-start | bytes 4866056 | tf_op jit(solution)/shard_map/ppermute | solution.py:57
  66.6 12.9 %collective-permute-start.10 = (bf16[288,2560]{1,0:T(8,128)(2,1)S(1)}, bf16[288,2560]{1,0:T(8,128)(2,1)S(1)}, u32[]{:S(2)}, u32[]{:S(2)}) collective-permute-start(bf16[288,2560]{1,0:T(8,128)(2,1)S(1)} %pad_maximum_fusion.2.refs_4_), channel_id=1, source_target_pairs={{0,4},{4,0},{8,12},{12,8},{16,20},{20,16},{24,28},{28,24},{1,5},{5... | collective-permute-start | bytes 4423688 | tf_op jit(solution)/shard_map/ppermute | solution.py:57
  78.5 7.5 %collective-permute-start.16 = (bf16[576,1024]{1,0:T(8,128)(2,1)S(1)}, bf16[576,1024]{1,0:T(8,128)(2,1)S(1)}, u32[]{:S(2)}, u32[]{:S(2)}) collective-permute-start(bf16[576,1024]{1,0:T(8,128)(2,1)S(1)} %pad_maximum_fusion.4.refs_2_.refs_15_), channel_id=1, source_target_pairs={{0,4},{4,0},{8,12},{12,8},{16,20},{20,16},{24,28},{28,24},{1,5},{5... | collective-permute-start | bytes 3538952 | tf_op jit(solution)/shard_map/ppermute | solution.py:57
  79.0 21.8 %collective-permute-start.17 = (bf16[144,2816]{1,0:T(8,128)(2,1)}, bf16[144,2816]{1,0:T(8,128)(2,1)S(1)}, u32[]{:S(2)}, u32[]{:S(2)}) collective-permute-start(bf16[144,2816]{1,0:T(8,128)(2,1)} %pad_maximum_fusion.7), channel_id=1, source_target_pairs={{0,16},{4,20},{8,24},{12,28},{16,0},{20,4},{24,8},{28,12},{1,17},{... | collective-permute-start | bytes 2433032 | tf_op jit(solution)/shard_map/ppermute | solution.py:57
  79.5 37.1 %collective-permute-start.18 = (bf16[144,2816]{1,0:T(8,128)(2,1)}, bf16[144,2816]{1,0:T(8,128)(2,1)S(1)}, u32[]{:S(2)}, u32[]{:S(2)}) collective-permute-start(bf16[144,2816]{1,0:T(8,128)(2,1)} %collective-permute-done.7), channel_id=1, source_target_pairs={{0,16},{4,20},{8,24},{12,28},{16,0},{20,4},{24,8},{28,12},{1,17},{... | collective-permute-start | bytes 2433032 | tf_op jit(solution)/shard_map/ppermute | solution.py:57
  81.0 19.7 %collective-permute-start.19 = (bf16[144,2560]{1,0:T(8,128)(2,1)}, bf16[144,2560]{1,0:T(8,128)(2,1)}, u32[]{:S(2)}, u32[]{:S(2)}) collective-permute-start(bf16[144,2560]{1,0:T(8,128)(2,1)} %pad_maximum_fusion.8), channel_id=1, source_target_pairs={{0,8},{4,12},{8,0},{12,4},{16,24},{20,28},{24,16},{28,20},{1,9},{5... | collective-permute-start | bytes 2211848 | tf_op jit(solution)/shard_map/ppermute | solution.py:57
  82.6 32.4 %collective-permute-start.20 = (bf16[144,2560]{1,0:T(8,128)(2,1)}, bf16[144,2560]{1,0:T(8,128)(2,1)S(1)}, u32[]{:S(2)}, u32[]{:S(2)}) collective-permute-start(bf16[144,2560]{1,0:T(8,128)(2,1)} %collective-permute-done.8), channel_id=1, source_target_pairs={{0,8},{4,12},{8,0},{12,4},{16,24},{20,28},{24,16},{28,20},{1,9},{5... | collective-permute-start | bytes 2211848 | tf_op jit(solution)/shard_map/ppermute | solution.py:57
  117.9 5.7 %collective-permute-start.22 = (bf16[288,2816]{1,0:T(8,128)(2,1)S(1)}, bf16[288,2816]{1,0:T(8,128)(2,1)S(1)}, u32[]{:S(2)}, u32[]{:S(2)}) collective-permute-start(bf16[288,2816]{1,0:T(8,128)(2,1)S(1)} %constant_dynamic-update-slice_fusion.refs_2_), channel_id=1, source_target_pairs={{0,4},{4,0},{8,12},{12,8},{16,20},{20,16},{24,28},{28,24},{1,5},{5... | collective-permute-start | bytes 4866056 | tf_op jit(solution)/shard_map/ppermute | solution.py:57
  119.1 26.7 %collective-permute-start.21 = (bf16[256,1152]{1,0:T(8,128)(2,1)S(1)}, bf16[256,1152]{1,0:T(8,128)(2,1)S(1)}, u32[]{:S(2)}, u32[]{:S(2)}) collective-permute-start(bf16[256,1152]{1,0:T(8,128)(2,1)S(1)} %copy-done.16), channel_id=1, source_target_pairs={{0,1},{1,0},{2,3},{3,2},{4,5},{5,4},{6,7},{7,6},{8,9},{9,8},{10,11... | collective-permute-start | bytes 1769480 | tf_op jit(solution)/shard_map/ppermute | solution.py:62
  120.4 42.4 %collective-permute-start.24 = (bf16[256,1152]{1,0:T(8,128)(2,1)S(1)}, bf16[256,1152]{1,0:T(8,128)(2,1)S(1)}, u32[]{:S(2)}, u32[]{:S(2)}) collective-permute-start(bf16[256,1152]{1,0:T(8,128)(2,1)S(1)} %copy-done.16), channel_id=1, source_target_pairs={{0,2},{1,3},{2,0},{3,1},{4,6},{5,7},{6,4},{7,5},{8,10},{9,11},{10,... | collective-permute-start | bytes 1769480 | tf_op jit(solution)/shard_map/ppermute | solution.py:62
  123.3 53.1 %collective-permute-start.25 = (bf16[256,1152]{1,0:T(8,128)(2,1)S(1)}, bf16[256,1152]{1,0:T(8,128)(2,1)}, u32[]{:S(2)}, u32[]{:S(2)}) collective-permute-start(bf16[256,1152]{1,0:T(8,128)(2,1)S(1)} %copy-done.16), channel_id=1, source_target_pairs={{0,3},{1,2},{2,1},{3,0},{4,7},{5,6},{6,5},{7,4},{8,11},{9,10},{10,... | collective-permute-start | bytes 1769480 | tf_op jit(solution)/shard_map/ppermute | solution.py:62
  176.4 30.5 %collective-permute-start.27 = (bf16[256,1152]{1,0:T(8,128)(2,1)}, bf16[256,1152]{1,0:T(8,128)(2,1)S(1)}, u32[]{:S(2)}, u32[]{:S(2)}) collective-permute-start(bf16[256,1152]{1,0:T(8,128)(2,1)} %get-tuple-element.240), channel_id=1, source_target_pairs={{0,2},{1,3},{2,0},{3,1},{4,6},{5,7},{6,4},{7,5},{8,10},{9,11},{10,... | collective-permute-start | bytes 1769480 | tf_op jit(solution)/shard_map/ppermute | solution.py:62
  176.5 30.4 %collective-permute-start.26 = (bf16[256,1152]{1,0:T(8,128)(2,1)S(1)}, bf16[256,1152]{1,0:T(8,128)(2,1)S(1)}, u32[]{:S(2)}, u32[]{:S(2)}) collective-permute-start(bf16[256,1152]{1,0:T(8,128)(2,1)S(1)} %copy-done.54), channel_id=1, source_target_pairs={{0,1},{1,0},{2,3},{3,2},{4,5},{5,4},{6,7},{7,6},{8,9},{9,8},{10,11... | collective-permute-start | bytes 1769480 | tf_op jit(solution)/shard_map/ppermute | solution.py:62
  207.8 5.6 %collective-permute-start.28 = (bf16[4,144,2560]{2,1,0:T(8,128)(2,1)}, bf16[4,144,2560]{2,1,0:T(8,128)(2,1)S(1)}, u32[]{:S(2)}, u32[]{:S(2)}) collective-permute-start(bf16[4,144,2560]{2,1,0:T(8,128)(2,1)} %get-tuple-element.249), channel_id=1, source_target_pairs={{0,4},{4,0},{8,12},{12,8},{16,20},{20,16},{24,28},{28,24},{1,5},{5... | collective-permute-start | bytes 8847368 | tf_op jit(solution)/shard_map/ppermute | solution.py:57
  207.8 26.4 %collective-permute-start.29 = (bf16[256,1152]{1,0:T(8,128)(2,1)}, bf16[256,1152]{1,0:T(8,128)(2,1)}, u32[]{:S(2)}, u32[]{:S(2)}) collective-permute-start(bf16[256,1152]{1,0:T(8,128)(2,1)} %get-tuple-element.255), channel_id=1, source_target_pairs={{0,3},{1,2},{2,1},{3,0},{4,7},{5,6},{6,5},{7,4},{8,11},{9,10},{10,... | collective-permute-start | bytes 1769480 | tf_op jit(solution)/shard_map/ppermute | solution.py:62
  234.2 6.2 %collective-permute-start.31 = (bf16[4,144,2816]{2,1,0:T(8,128)(2,1)}, bf16[4,144,2816]{2,1,0:T(8,128)(2,1)}, u32[]{:S(2)}, u32[]{:S(2)}) collective-permute-start(bf16[4,144,2816]{2,1,0:T(8,128)(2,1)} %get-tuple-element.265), channel_id=1, source_target_pairs={{0,4},{4,0},{8,12},{12,8},{16,20},{20,16},{24,28},{28,24},{1,5},{5... | collective-permute-start | bytes 9732104 | tf_op jit(solution)/shard_map/ppermute | solution.py:57
  235.1 44.9 %collective-permute-start.33 = (bf16[2,144,2560]{2,1,0:T(8,128)(2,1)}, bf16[2,144,2560]{2,1,0:T(8,128)(2,1)S(1)}, u32[]{:S(2)}, u32[]{:S(2)}) collective-permute-start(bf16[2,144,2560]{2,1,0:T(8,128)(2,1)} %get-tuple-element.358), channel_id=1, source_target_pairs={{0,16},{4,20},{8,24},{12,28},{16,0},{20,4},{24,8},{28,12},{1,17},{... | collective-permute-start | bytes 4423688 | tf_op jit(solution)/shard_map/ppermute | solution.py:57
  236.8 28.5 %collective-permute-start.30 = (bf16[512,1152]{1,0:T(8,128)(2,1)S(1)}, bf16[512,1152]{1,0:T(8,128)(2,1)S(1)}, u32[]{:S(2)}, u32[]{:S(2)}) collective-permute-start(bf16[512,1152]{1,0:T(8,128)(2,1)S(1)} %pad_maximum_fusion.5), channel_id=1, source_target_pairs={{0,1},{1,0},{2,3},{3,2},{4,5},{5,4},{6,7},{7,6},{8,9},{9,8},{10,11... | collective-permute-start | bytes 3538952 | tf_op jit(solution)/shard_map/ppermute | solution.py:62
  245.5 48.4 %collective-permute-start.34 = (bf16[2,144,2816]{2,1,0:T(8,128)(2,1)}, bf16[2,144,2816]{2,1,0:T(8,128)(2,1)}, u32[]{:S(2)}, u32[]{:S(2)}) collective-permute-start(bf16[2,144,2816]{2,1,0:T(8,128)(2,1)} %get-tuple-element.356), channel_id=1, source_target_pairs={{0,8},{4,12},{8,0},{12,4},{16,24},{20,28},{24,16},{28,20},{1,9},{5... | collective-permute-start | bytes 4866056 | tf_op jit(solution)/shard_map/ppermute | solution.py:57
  278.3 13.9 %collective-permute-start.32 = (bf16[512,512]{1,0:T(8,128)(2,1)}, bf16[512,512]{1,0:T(8,128)(2,1)S(1)}, u32[]{:S(2)}, u32[]{:S(2)}) collective-permute-start(bf16[512,512]{1,0:T(8,128)(2,1)} %pad_maximum_fusion.11), channel_id=1, source_target_pairs={{0,1},{1,0},{2,3},{3,2},{4,5},{5,4},{6,7},{7,6},{8,9},{9,8},{10,11... | collective-permute-start | bytes 1572872 | tf_op jit(solution)/shard_map/ppermute | solution.py:62
  292.3 13.7 %collective-permute-start.40 = (bf16[256,512]{1,0:T(8,128)(2,1)S(1)}, bf16[256,512]{1,0:T(8,128)(2,1)S(1)}, u32[]{:S(2)}, u32[]{:S(2)}) collective-permute-start(bf16[256,512]{1,0:T(8,128)(2,1)S(1)} %add_convert_fusion.10), channel_id=1, source_target_pairs={{0,2},{1,3},{2,0},{3,1},{4,6},{5,7},{6,4},{7,5},{8,10},{9,11},{10,... | collective-permute-start | bytes 786440 | tf_op jit(solution)/shard_map/ppermute | solution.py:62
  293.8 16.6 %collective-permute-start.35 = (bf16[4,144,1408]{2,1,0:T(8,128)(2,1)S(1)}, bf16[4,144,1408]{2,1,0:T(8,128)(2,1)S(1)}, u32[]{:S(2)}, u32[]{:S(2)}) collective-permute-start(bf16[4,144,1408]{2,1,0:T(8,128)(2,1)S(1)} %copy-done.52), channel_id=1, source_target_pairs={{0,4},{4,0},{8,12},{12,8},{16,20},{20,16},{24,28},{28,24},{1,5},{5... | collective-permute-start | bytes 4866056 | tf_op jit(solution)/shard_map/ppermute | solution.py:57
  293.9 16.6 %collective-permute-start.36 = (bf16[4,144,1280]{2,1,0:T(8,128)(2,1)S(1)}, bf16[4,144,1280]{2,1,0:T(8,128)(2,1)S(1)}, u32[]{:S(2)}, u32[]{:S(2)}) collective-permute-start(bf16[4,144,1280]{2,1,0:T(8,128)(2,1)S(1)} %copy-done.53), channel_id=1, source_target_pairs={{0,4},{4,0},{8,12},{12,8},{16,20},{20,16},{24,28},{28,24},{1,5},{5... | collective-permute-start | bytes 4423688 | tf_op jit(solution)/shard_map/ppermute | solution.py:57
  294.5 35.7 %collective-permute-start.47 = (bf16[144,2560]{1,0:T(8,128)(2,1)S(1)}, bf16[144,2560]{1,0:T(8,128)(2,1)S(1)}, u32[]{:S(2)}, u32[]{:S(2)}) collective-permute-start(bf16[144,2560]{1,0:T(8,128)(2,1)S(1)} %get-tuple-element.368), channel_id=1, source_target_pairs={{0,8},{4,12},{8,0},{12,4},{16,24},{20,28},{24,16},{28,20},{1,9},{5... | collective-permute-start | bytes 2211848 | tf_op jit(solution)/shard_map/ppermute | solution.py:57
  308.8 21.1 %collective-permute-start.46 = (bf16[144,2816]{1,0:T(8,128)(2,1)S(1)}, bf16[144,2816]{1,0:T(8,128)(2,1)S(1)}, u32[]{:S(2)}, u32[]{:S(2)}) collective-permute-start(bf16[144,2816]{1,0:T(8,128)(2,1)S(1)} %get-tuple-element.364), channel_id=1, source_target_pairs={{0,16},{4,20},{8,24},{12,28},{16,0},{20,4},{24,8},{28,12},{1,17},{... | collective-permute-start | bytes 2433032 | tf_op jit(solution)/shard_map/ppermute | solution.py:57
  311.8 36.3 %collective-permute-start.38 = (bf16[2,144,1280]{2,1,0:T(8,128)(2,1)}, bf16[2,144,1280]{2,1,0:T(8,128)(2,1)}, u32[]{:S(2)}, u32[]{:S(2)}) collective-permute-start(bf16[2,144,1280]{2,1,0:T(8,128)(2,1)} %get-tuple-element.371), channel_id=1, source_target_pairs={{0,16},{4,20},{8,24},{12,28},{16,0},{20,4},{24,8},{28,12},{1,17},{... | collective-permute-start | bytes 2211848 | tf_op jit(solution)/shard_map/ppermute | solution.py:57
  314.4 33.7 %collective-permute-start.37 = (bf16[2,144,1408]{2,1,0:T(8,128)(2,1)}, bf16[2,144,1408]{2,1,0:T(8,128)(2,1)S(1)}, u32[]{:S(2)}, u32[]{:S(2)}) collective-permute-start(bf16[2,144,1408]{2,1,0:T(8,128)(2,1)} %get-tuple-element.367), channel_id=1, source_target_pairs={{0,8},{4,12},{8,0},{12,4},{16,24},{20,28},{24,16},{28,20},{1,9},{5... | collective-permute-start | bytes 2433032 | tf_op jit(solution)/shard_map/ppermute | solution.py:57
  349.4 7.6 %collective-permute-start.43 = (bf16[144,1280]{1,0:T(8,128)(2,1)S(1)}, bf16[144,1280]{1,0:T(8,128)(2,1)S(1)}, u32[]{:S(2)}, u32[]{:S(2)}) collective-permute-start(bf16[144,1280]{1,0:T(8,128)(2,1)S(1)} %dynamic-slice_bitcast_fusion.13), channel_id=1, source_target_pairs={{0,8},{4,12},{8,0},{12,4},{16,24},{20,28},{24,16},{28,20},{1,9},{5... | collective-permute-start | bytes 1105928 | tf_op jit(solution)/shard_map/ppermute | solution.py:57
  350.3 8.0 %collective-permute-start.41 = (bf16[144,1408]{1,0:T(8,128)(2,1)S(1)}, bf16[144,1408]{1,0:T(8,128)(2,1)S(1)}, u32[]{:S(2)}, u32[]{:S(2)}) collective-permute-start(bf16[144,1408]{1,0:T(8,128)(2,1)S(1)} %dynamic-slice_bitcast_fusion.12), channel_id=1, source_target_pairs={{0,16},{4,20},{8,24},{12,28},{16,0},{20,4},{24,8},{28,12},{1,17},{... | collective-permute-start | bytes 1216520 | tf_op jit(solution)/shard_map/ppermute | solution.py:57
  352.1 44.3 %collective-permute-start.39 = (bf16[256,1152]{1,0:T(8,128)(2,1)S(1)}, bf16[256,1152]{1,0:T(8,128)(2,1)S(1)}, u32[]{:S(2)}, u32[]{:S(2)}) collective-permute-start(bf16[256,1152]{1,0:T(8,128)(2,1)S(1)} %add_convert_fusion.8), channel_id=1, source_target_pairs={{0,2},{1,3},{2,0},{3,1},{4,6},{5,7},{6,4},{7,5},{8,10},{9,11},{10,... | collective-permute-start | bytes 1769480 | tf_op jit(solution)/shard_map/ppermute | solution.py:62
  358.6 8.4 %collective-permute-start.48 = (bf16[36,640]{1,0:T(8,128)(2,1)S(1)}, bf16[36,640]{1,0:T(8,128)(2,1)S(1)}, u32[]{:S(2)}, u32[]{:S(2)}) collective-permute-start(bf16[36,640]{1,0:T(8,128)(2,1)S(1)} %get-tuple-element.380), channel_id=1, source_target_pairs={{0,1},{1,0},{2,3},{3,2},{4,5},{5,4},{6,7},{7,6},{8,9},{9,8},{10,11... | collective-permute-start | bytes 138248 | tf_op jit(solution)/shard_map/ppermute | solution.py:62
  358.7 27.2 %collective-permute-start.49 = (bf16[36,640]{1,0:T(8,128)(2,1)S(1)}, bf16[36,640]{1,0:T(8,128)(2,1)S(1)}, u32[]{:S(2)}, u32[]{:S(2)}) collective-permute-start(bf16[36,640]{1,0:T(8,128)(2,1)S(1)} %get-tuple-element.381), channel_id=1, source_target_pairs={{0,2},{1,3},{2,0},{3,1},{4,6},{5,7},{6,4},{7,5},{8,10},{9,11},{10,... | collective-permute-start | bytes 138248 | tf_op jit(solution)/shard_map/ppermute | solution.py:62
  360.8 25.1 %collective-permute-start.50 = (bf16[36,640]{1,0:T(8,128)(2,1)S(1)}, bf16[36,640]{1,0:T(8,128)(2,1)S(1)}, u32[]{:S(2)}, u32[]{:S(2)}) collective-permute-start(bf16[36,640]{1,0:T(8,128)(2,1)S(1)} %get-tuple-element.382), channel_id=1, source_target_pairs={{0,3},{1,2},{2,1},{3,0},{4,7},{5,6},{6,5},{7,4},{8,11},{9,10},{10,... | collective-permute-start | bytes 138248 | tf_op jit(solution)/shard_map/ppermute | solution.py:62
  363.1 27.8 %collective-permute-start.44 = (bf16[144,512]{1,0:T(8,128)(2,1)S(1)}, bf16[144,512]{1,0:T(8,128)(2,1)S(1)}, u32[]{:S(2)}, u32[]{:S(2)}) collective-permute-start(bf16[144,512]{1,0:T(8,128)(2,1)S(1)} %get-tuple-element.383), channel_id=1, source_target_pairs={{0,2},{1,3},{2,0},{3,1},{4,6},{5,7},{6,4},{7,5},{8,10},{9,11},{10,... | collective-permute-start | bytes 442376 | tf_op jit(solution)/shard_map/ppermute | solution.py:62
  367.0 23.9 %collective-permute-start.45 = (bf16[144,512]{1,0:T(8,128)(2,1)S(1)}, bf16[144,512]{1,0:T(8,128)(2,1)S(1)}, u32[]{:S(2)}, u32[]{:S(2)}) collective-permute-start(bf16[144,512]{1,0:T(8,128)(2,1)S(1)} %get-tuple-element.384), channel_id=1, source_target_pairs={{0,3},{1,2},{2,1},{3,0},{4,7},{5,6},{6,5},{7,4},{8,11},{9,10},{10,... | collective-permute-start | bytes 442376 | tf_op jit(solution)/shard_map/ppermute | solution.py:62
  385.9 7.3 %collective-permute-start.42 = (bf16[144,512]{1,0:T(8,128)(2,1)S(1)}, bf16[144,512]{1,0:T(8,128)(2,1)S(1)}, u32[]{:S(2)}, u32[]{:S(2)}) collective-permute-start(bf16[144,512]{1,0:T(8,128)(2,1)S(1)} %slice.321), channel_id=1, source_target_pairs={{0,1},{1,0},{2,3},{3,2},{4,5},{5,4},{6,7},{7,6},{8,9},{9,8},{10,11... | collective-permute-start | bytes 442376 | tf_op jit(solution)/shard_map/ppermute | solution.py:62
  (58 other events, 540.2 us)
